TPU v7x, 32 devices: a whole 2x2x4 slice. The times are simulated.
32 devices in a mesh: dp: 4 (over y, x), wide: 8 (over z, core).
Axes of the slice: x: 2, y: 2, z: 4, core: 2. Of those that a mesh axis runs over, the one named last changes fastest.
Arguments:
- source_ids: int32 [32, 256], replicated, may hold values from 0 to 32767
- token_ids: int32 [32, 256], replicated, may hold values from 0 to 32767
- targets: int32 [32, 256], replicated, may hold values from 0 to 32767
- pad_mask: int32 [32, 256], replicated, may hold values from 0 to 1, as said below
- pass_widths: int32 [2], replicated, may hold values from 768 to 3072, as said below
- attn_master: float32 [3, 640, 2048], P(None, ('dp', 'wide'))
- attn_m: float32 [3, 640, 2048], P(None, ('dp', 'wide')), may hold values from -5.9604645e-07 to 5.9604645e-07
- attn_v: float32 [3, 640, 2048], P(None, ('dp', 'wide'))
- norm_params: float32 [14, 640], replicated
- norm_m: float32 [14, 640], replicated, may hold values from -2.861023e-06 to 2.861023e-06
- norm_v: float32 [14, 640], replicated
- up_master: float32 [2, 640, 3072], P(None, None, 'wide'), may hold values from -0.25 to 0.25
- up_m: float32 [2, 640, 3072], P(None, None, 'wide'), may hold values from -5.9604645e-07 to 5.9604645e-07
- up_v: float32 [2, 640, 3072], P(None, None, 'wide')
- down_master: float32 [2, 3072, 640], P(None, 'wide'), may hold values from -0.21875 to 0.21875
- down_m: float32 [2, 3072, 640], P(None, 'wide'), may hold values from -5.9604645e-07 to 5.9604645e-07
- down_v: float32 [2, 3072, 640], P(None, 'wide')
- embed_master: float32 [32768, 640], P('wide'), may hold values from -0.25 to 0.25
- embed_m: float32 [32768, 640], P('wide'), may hold values from -5.9604645e-07 to 5.9604645e-07
- embed_v: float32 [32768, 640], P('wide')
- ema_old: float32 [32768, 640], P('wide', 'dp'), may hold values from -0.25 to 0.25
Outputs:
- losses: float32 [2], replicated
- row_losses: float32 [2, 32, 256], P(None, ('dp', 'wide'))
- grad_norm: float32 [1], replicated
- attn_new: float32 [3, 640, 2048], P(None, ('dp', 'wide'))
- attn_m_new: float32 [3, 640, 2048], P(None, ('dp', 'wide'))
- attn_v_new: float32 [3, 640, 2048], P(None, ('dp', 'wide'))
- norm_new: float32 [14, 640], replicated
- norm_m_new: float32 [14, 640], replicated
- norm_v_new: float32 [14, 640], replicated
- up_new: float32 [2, 640, 3072], P(None, None, 'wide')
- up_m_new: float32 [2, 640, 3072], P(None, None, 'wide')
- up_v_new: float32 [2, 640, 3072], P(None, None, 'wide')
- down_new: float32 [2, 3072, 640], P(None, 'wide')
- down_m_new: float32 [2, 3072, 640], P(None, 'wide')
- down_v_new: float32 [2, 3072, 640], P(None, 'wide')
- embed_new: float32 [32768, 640], P('wide')
- embed_m_new: float32 [32768, 640], P('wide')
- embed_v_new: float32 [32768, 640], P('wide')
- ema_new: float32 [32768, 640], P('wide', 'dp')
- attn_half: bfloat16 [3, 640, 2048], P(None, ('dp', 'wide'))
- up_half: bfloat16 [2, 640, 3072], P(None, None, 'wide')
- down_half: bfloat16 [2, 3072, 640], P(None, 'wide')
- embed_half: bfloat16 [32768, 640], P('wide')
Inputs may be any that keep to these rules, and one draw needn't show every extreme that they name: `pad_mask`: each pair's mask is 1 on a prefix of 64 or more positions and 0 after it; it serves the source and the target alike. `pass_widths`: entry 0 is 3072; entry 1 is a multiple of 8 from 768 to 1536.
All inputs are finite; a program needn't handle non-finite values.
Results may differ from a plain program's by a relative error of at most 0.0067.
Values may be sent and summed in bfloat16 or wider, within the bound.
A program may use at most 320 MiB of HBM per device.

v0:
```python
import math

import jax
import jax.numpy as jnp
from jax import lax
from jax.sharding import PartitionSpec as P

HEADS = 8
HEAD = 64
V = 32768


smooth = 0.1
norm_eps = 1e-05
clip_limit = 0.005
beta_first = 0.9
beta_second = 0.98
adam_eps = 1e-08
rate_matrix = 0.02
rate_gains = 0.2
decay_weight = 0.01
ema_decay = 0.8
norm_count = 7


def merged(part, axis, combine):
    gathered = jax.tree.map(lambda a: lax.all_gather(a, axis), part)

    def take(source):
        return jax.tree.map(lambda a: lax.dynamic_index_in_dim(a, source, 0, False), gathered)

    return lax.fori_loop(
        1, lax.axis_size(axis), lambda source, state: combine(state, take(source)), take(0)
    )


def dot_rows(left, right):
    return lax.dot_general(
        left, right, (((1,), (1,)), ((), ())), preferred_element_type=jnp.float32
    )


def dot_cols(left, right):
    return lax.dot_general(
        left, right, (((0,), (0,)), ((), ())), preferred_element_type=jnp.float32
    )


def sinusoid(length, model_width):
    places = jnp.arange(length, dtype=jnp.float32)[:, None]
    halves = jnp.arange(model_width // 2, dtype=jnp.float32)[None, :]
    angles = places * jnp.exp(halves * (-2.0 * math.log(10000.0) / model_width))
    return jnp.concatenate([jnp.sin(angles), jnp.cos(angles)], axis=1)


def layer_norm(values, gain, shift):
    centered = values - jnp.mean(values, axis=-1, keepdims=True)
    inverse = lax.rsqrt(jnp.mean(centered * centered, axis=-1, keepdims=True) + norm_eps)
    normed = centered * inverse
    return (normed * gain + shift, (normed, inverse))


def norm_back(upstream, stats, gain):
    normed, inverse = stats
    scaled = upstream * gain
    back = inverse * (
        scaled
        - jnp.mean(scaled, axis=-1, keepdims=True)
        - normed * jnp.mean(scaled * normed, axis=-1, keepdims=True)
    )
    return (back, jnp.sum(upstream * normed, axis=0), jnp.sum(upstream, axis=0))


def masked_scores(queries, key_rows, allowed):
    scores = jnp.einsum(
        "sqhe,skhe->shqk", queries, key_rows, preferred_element_type=jnp.float32
    ) * HEAD ** (-0.5)
    return jnp.where(allowed, scores, -1e30)


def attn_forward(q_in, kv_in, block, allowed, seq_dev):
    tokens = q_in.shape[0]
    width = block.shape[1] // 4
    queries = jnp.dot(q_in, block[:, :width], preferred_element_type=jnp.float32).astype(
        jnp.bfloat16
    )
    queries = queries.reshape(seq_dev, -1, HEADS, HEAD)
    pair = jnp.dot(kv_in, block[:, width : 3 * width], preferred_element_type=jnp.float32).astype(
        jnp.bfloat16
    )
    key_rows = pair[:, :width].reshape(seq_dev, -1, HEADS, HEAD)
    value_rows = pair[:, width:].reshape(seq_dev, -1, HEADS, HEAD)
    scores = masked_scores(queries, key_rows, allowed)
    row_peak = jnp.max(scores, axis=-1, keepdims=True)
    row_exp = jnp.exp(scores - row_peak)
    row_total = jnp.sum(row_exp, axis=-1, keepdims=True)
    log_total = row_peak + jnp.log(row_total)
    probs_low = (row_exp / row_total).astype(jnp.bfloat16)
    mixed_low = jnp.einsum(
        "shqk,skhe->sqhe", probs_low, value_rows, preferred_element_type=jnp.float32
    )
    mixed_low = mixed_low.reshape(tokens, width).astype(jnp.bfloat16)
    output = dot_rows(mixed_low, block[:, 3 * width :])
    return (output, (q_in, kv_in, queries, key_rows, value_rows, log_total, mixed_low, allowed))


def attention_backward_pass(kept, grad_low, block):
    q_in, kv_in, queries, key_rows, value_rows, log_total, mixed_low, allowed = kept
    tokens = q_in.shape[0]
    width = block.shape[1] // 4
    out_weight_grad = dot_cols(grad_low, mixed_low)
    mixed_grad = jnp.dot(
        grad_low, block[:, 3 * width :], preferred_element_type=jnp.float32
    ).astype(jnp.bfloat16)
    mixed_grad = mixed_grad.reshape(queries.shape)
    probs = jnp.exp(masked_scores(queries, key_rows, allowed) - log_total)
    probs_grad = jnp.einsum(
        "sqhe,skhe->shqk", mixed_grad, value_rows, preferred_element_type=jnp.float32
    )
    value_grad = jnp.einsum(
        "shqk,sqhe->skhe",
        probs.astype(jnp.bfloat16),
        mixed_grad,
        preferred_element_type=jnp.float32,
    )
    score_low = (probs * (probs_grad - jnp.sum(probs * probs_grad, axis=-1, keepdims=True))).astype(
        jnp.bfloat16
    )
    query_grad = jnp.einsum(
        "shqk,skhe->sqhe", score_low, key_rows, preferred_element_type=jnp.float32
    ) * HEAD ** (-0.5)
    key_grad = jnp.einsum(
        "shqk,sqhe->skhe", score_low, queries, preferred_element_type=jnp.float32
    ) * HEAD ** (-0.5)
    query_low = query_grad.reshape(tokens, width).astype(jnp.bfloat16)
    pair_low = jnp.concatenate(
        [key_grad.reshape(tokens, width), value_grad.reshape(tokens, width)], axis=1
    ).astype(jnp.bfloat16)
    block_grad = jnp.concatenate(
        [dot_cols(q_in, query_low), dot_cols(kv_in, pair_low), out_weight_grad], axis=1
    )
    return (
        dot_rows(query_low, block[:, :width]),
        dot_rows(pair_low, block[:, width : 3 * width]),
        block_grad,
    )


def ffn_pass(hidden, inner, down, width_now):
    units = jnp.arange(inner.shape[1])[None, :]
    active = (units < width_now) & (inner > 0)
    act_low = jnp.where(active, inner, 0.0).astype(jnp.bfloat16)
    return (hidden + jnp.dot(act_low, down, preferred_element_type=jnp.float32), active, act_low)


def head_stats(head_in, row_targets, table_part, offset):
    row_count = head_in.shape[0]
    block_rows = math.gcd(row_count, 512)
    columns = offset + jnp.arange(table_part.shape[0])

    def one_block(block_items):
        rows_low, block_targets = block_items
        logits = dot_rows(rows_low, table_part)
        row_peak = jnp.max(logits, axis=-1)
        row_total = jnp.sum(jnp.exp(logits - row_peak[:, None]), axis=-1)
        target_logit = jnp.sum(
            jnp.where(columns[None, :] == block_targets[:, None], logits, 0.0), axis=-1
        )
        return (row_peak, row_total, target_logit, jnp.sum(logits, axis=-1))

    results = lax.map(
        one_block,
        (head_in.reshape(-1, block_rows, head_in.shape[1]), row_targets.reshape(-1, block_rows)),
    )
    return tuple((stat_part.reshape(-1) for stat_part in results))


def head_grads(head_in, row_targets, row_weights, log_total, table_part, offset):
    row_count, model_width = head_in.shape
    block_rows = math.gcd(row_count, 512)
    columns = offset + jnp.arange(table_part.shape[0])

    def one_block(table_grad, block_items):
        rows_low, block_targets, block_weights, block_lse = block_items
        probs = jnp.exp(dot_rows(rows_low, table_part) - block_lse[:, None])
        hits = columns[None, :] == block_targets[:, None]
        logit_low = (
            block_weights[:, None] * (jnp.where(hits, probs - (1.0 - smooth), probs) - smooth / V)
        ).astype(jnp.bfloat16)
        return (
            table_grad + dot_cols(logit_low, rows_low),
            jnp.dot(logit_low, table_part, preferred_element_type=jnp.float32),
        )

    block_items = (
        head_in.reshape(-1, block_rows, model_width),
        row_targets.reshape(-1, block_rows),
        row_weights.reshape(-1, block_rows),
        log_total.reshape(-1, block_rows),
    )
    table_grad, row_grads = lax.scan(
        one_block, jnp.zeros(table_part.shape, jnp.float32), block_items
    )
    return (row_grads.reshape(row_count, model_width), table_grad)


def join_stats(first_part, second_part):
    row_peak = jnp.maximum(first_part[0], second_part[0])
    row_total = first_part[1] * jnp.exp(first_part[0] - row_peak) + second_part[1] * jnp.exp(
        second_part[0] - row_peak
    )
    return (row_peak, row_total, first_part[2] + second_part[2], first_part[3] + second_part[3])


def adamw(weight, first_m, second_m, grad_item, step_rate):
    first_new = beta_first * first_m + (1.0 - beta_first) * grad_item
    second_new = beta_second * second_m + (1.0 - beta_second) * grad_item * grad_item
    weight_new = weight - step_rate * (
        first_new / (jnp.sqrt(second_new) + adam_eps) + decay_weight * weight
    )
    return (weight_new, first_new, second_new)


def rows_of(source, row_start, number):
    return lax.dynamic_slice_in_dim(source, row_start, number, 0).reshape(-1)


def local(
    source_ids,
    token_ids,
    targets,
    pad_mask,
    pass_widths,
    attn_master,
    attn_m,
    attn_v,
    norm_params,
    norm_m,
    norm_v,
    up_master,
    up_m,
    up_v,
    down_master,
    down_m,
    down_v,
    embed_master,
    embed_m,
    embed_v,
    ema_old,
):
    wide_count = lax.axis_size("wide")
    wide_at = lax.axis_index("wide")
    dp_count = lax.axis_size("dp")
    dp_at = lax.axis_index("dp")
    model_width = norm_params.shape[1]
    length = token_ids.shape[1]
    seq_dev = token_ids.shape[0] // (wide_count * dp_count)
    tokens = seq_dev * length
    vocab_shard = embed_master.shape[0]
    attn_full = lax.all_gather(attn_master.astype(jnp.bfloat16), ("dp", "wide"), axis=1, tiled=True)
    up_full, down_full = (
        lax.all_gather(up_master.astype(jnp.bfloat16), "wide", axis=2, tiled=True),
        lax.all_gather(down_master.astype(jnp.bfloat16), "wide", axis=1, tiled=True),
    )
    table_local = embed_master.astype(jnp.bfloat16)
    group_start = dp_at * wide_count * seq_dev
    own_start = group_start + wide_at * seq_dev
    count_all = jnp.sum(pad_mask).astype(jnp.float32)
    group_src = rows_of(source_ids, group_start, wide_count * seq_dev).reshape(wide_count, tokens)
    group_tgt = rows_of(token_ids, group_start, wide_count * seq_dev).reshape(wide_count, tokens)
    group_ids = jnp.concatenate([group_src, group_tgt], axis=1).reshape(-1)
    own_mask = rows_of(pad_mask, own_start, seq_dev).reshape(seq_dev, length) > 0
    free_mask = own_mask[:, None, None, :]
    causal = jnp.arange(length)[:, None] >= jnp.arange(length)[None, :]
    causal_mask = free_mask & causal[None, None]
    offset = wide_at * vocab_shard
    picked = group_ids - offset
    inside = (picked >= 0) & (picked < vocab_shard)
    found_rows = jnp.take(table_local, jnp.clip(picked, 0, vocab_shard - 1), axis=0).astype(
        jnp.float32
    )
    embedded = lax.psum_scatter(
        jnp.where(inside[:, None], found_rows, 0.0).astype(jnp.bfloat16),
        "wide",
        scatter_dimension=0,
        tiled=True,
    ).astype(jnp.float32)
    position = jnp.tile(sinusoid(length, model_width), (seq_dev, 1))
    src_in = math.sqrt(model_width) * embedded[:tokens] + position
    tgt_in = math.sqrt(model_width) * embedded[tokens:] + position

    def norm_at(values, index):
        return layer_norm(values, norm_params[index], norm_params[norm_count + index])

    src_val, source_norm_statistics = norm_at(src_in, 0)
    src_low = src_val.astype(jnp.bfloat16)
    src_att, src_kept = attn_forward(src_low, src_low, attn_full[0], free_mask, seq_dev)
    src_hidden = src_in + src_att
    sff_val, sff_stats = norm_at(src_hidden, 1)
    sff_low = sff_val.astype(jnp.bfloat16)
    src_inner = jnp.dot(sff_low, up_full[0], preferred_element_type=jnp.float32)
    tgt_val, tgt_stats = norm_at(tgt_in, 3)
    tgt_low = tgt_val.astype(jnp.bfloat16)
    tgt_att, tgt_kept = attn_forward(tgt_low, tgt_low, attn_full[1], causal_mask, seq_dev)
    tgt_hidden = tgt_in + tgt_att
    cross_val, cross_stats = norm_at(tgt_hidden, 4)
    cross_low = cross_val.astype(jnp.bfloat16)
    passes = []
    final_list = []
    for pass_index in range(2):
        enc_out, enc_active, enc_act = ffn_pass(
            src_hidden, src_inner, down_full[0], pass_widths[pass_index]
        )
        mem_val, mem_stats = norm_at(enc_out, 2)
        mem_low = mem_val.astype(jnp.bfloat16)
        x_att, x_kept = attn_forward(cross_low, mem_low, attn_full[2], free_mask, seq_dev)
        crossed = tgt_hidden + x_att
        dff_val, dff_stats = norm_at(crossed, 5)
        dff_low = dff_val.astype(jnp.bfloat16)
        dec_inner = jnp.dot(dff_low, up_full[1], preferred_element_type=jnp.float32)
        dec_out, dec_active, dec_act = ffn_pass(
            crossed, dec_inner, down_full[1], pass_widths[pass_index]
        )
        fin_val, fin_stats = norm_at(dec_out, 6)
        passes.append(
            (
                enc_active,
                enc_act,
                mem_stats,
                x_kept,
                dff_stats,
                dff_low,
                dec_active,
                dec_act,
                fin_stats,
            )
        )
        final_list.append(fin_val.astype(jnp.bfloat16))
    final_pair = (final_list[0], final_list[1])
    gathered = (
        lax.all_gather(final_pair[0], "wide", axis=0, tiled=True),
        lax.all_gather(final_pair[1], "wide", axis=0, tiled=True),
    )
    head_in = jnp.concatenate(gathered, axis=0)
    row_targets = jnp.tile(rows_of(targets, group_start, wide_count * seq_dev), 2)
    row_masks = jnp.tile(
        rows_of(pad_mask, group_start, wide_count * seq_dev).astype(jnp.float32), 2
    )
    row_stats = head_stats(head_in, row_targets, table_local, offset)
    row_peak, row_total, target_logit, logit_sum = merged(row_stats, "wide", join_stats)
    row_weights = row_masks / count_all
    log_total = row_peak + jnp.log(row_total)
    row_error = log_total - (1.0 - smooth) * target_logit - smooth / V * logit_sum
    row_loss = (row_weights * row_error).reshape(2, -1)
    row_plain = (row_masks * row_error).reshape(2, -1)
    row_grads, table_grad = head_grads(
        head_in, row_targets, row_weights, log_total, table_local, offset
    )
    half_rows = head_in.shape[0] // 2
    loss_own = jnp.sum(lax.dynamic_slice_in_dim(row_loss, wide_at * tokens, tokens, 1), axis=1)
    plain_own = lax.dynamic_slice_in_dim(row_plain, wide_at * tokens, tokens, 1)
    final_grads = (
        lax.psum_scatter(row_grads[:half_rows], "wide", scatter_dimension=0, tiled=True),
        lax.psum_scatter(row_grads[half_rows:], "wide", scatter_dimension=0, tiled=True),
    )
    row_losses = plain_own.reshape(2, seq_dev, length)
    gain_parts = [jnp.zeros((model_width,), jnp.float32) for index in range(norm_count)]
    shift_parts = [jnp.zeros((model_width,), jnp.float32) for index in range(norm_count)]

    def backward_layer_norm(upstream, stats, index):
        back, gain_part, shift_part = norm_back(upstream, stats, norm_params[index])
        gain_parts[index] = gain_parts[index] + gain_part
        shift_parts[index] = shift_parts[index] + shift_part
        return back

    src_inner_grad = jnp.zeros(src_inner.shape, jnp.float32)
    source_hidden_gradient = jnp.zeros((tokens, model_width), jnp.float32)
    tgt_hidden_grad = jnp.zeros((tokens, model_width), jnp.float32)
    cross_grad = jnp.zeros((tokens, model_width), jnp.float32)
    cross_weight = jnp.zeros(attn_full.shape[1:], jnp.float32)
    up_grads = [jnp.zeros(up_full.shape[1:], jnp.float32) for index in range(2)]
    down_grads = [jnp.zeros(down_full.shape[1:], jnp.float32) for index in range(2)]
    for pass_index in range(2):
        (
            enc_active,
            enc_act,
            mem_stats,
            x_kept,
            dff_stats,
            dff_low,
            dec_active,
            dec_act,
            fin_stats,
        ) = passes[pass_index]
        out_grad = backward_layer_norm(final_grads[pass_index], fin_stats, 6)
        out_low = out_grad.astype(jnp.bfloat16)
        down_grads[1] = down_grads[1] + dot_cols(dec_act, out_low)
        dec_low = jnp.where(dec_active, dot_rows(out_low, down_full[1]), 0.0).astype(jnp.bfloat16)
        up_grads[1] = up_grads[1] + dot_cols(dff_low, dec_low)
        crossed_grad = out_grad + backward_layer_norm(dot_rows(dec_low, up_full[1]), dff_stats, 5)
        query_in, memory_in, block_grad = attention_backward_pass(
            x_kept, crossed_grad.astype(jnp.bfloat16), attn_full[2]
        )
        cross_weight = cross_weight + block_grad
        tgt_hidden_grad = tgt_hidden_grad + crossed_grad
        cross_grad = cross_grad + query_in
        enc_grad = backward_layer_norm(memory_in, mem_stats, 2)
        enc_low = enc_grad.astype(jnp.bfloat16)
        down_grads[0] = down_grads[0] + dot_cols(enc_act, enc_low)
        src_inner_grad = src_inner_grad + jnp.where(
            enc_active, dot_rows(enc_low, down_full[0]), 0.0
        )
        source_hidden_gradient = source_hidden_gradient + enc_grad
    tgt_hidden_grad = tgt_hidden_grad + backward_layer_norm(cross_grad, cross_stats, 4)
    src_inner_low = src_inner_grad.astype(jnp.bfloat16)
    up_grads[0] = dot_cols(sff_low, src_inner_low)
    source_hidden_gradient = source_hidden_gradient + backward_layer_norm(
        dot_rows(src_inner_low, up_full[0]), sff_stats, 1
    )
    tq_in, tkv_in, tgt_weight = attention_backward_pass(
        tgt_kept, tgt_hidden_grad.astype(jnp.bfloat16), attn_full[1]
    )
    tgt_in_grad = tgt_hidden_grad + backward_layer_norm(tq_in + tkv_in, tgt_stats, 3)
    source_query_input, source_key_value_input, source_norm_weight = attention_backward_pass(
        src_kept, source_hidden_gradient.astype(jnp.bfloat16), attn_full[0]
    )
    source_input_gradient = source_hidden_gradient + backward_layer_norm(
        source_query_input + source_key_value_input, source_norm_statistics, 0
    )
    attn_grad = jnp.stack([source_norm_weight, tgt_weight, cross_weight])
    up_grad = jnp.stack(up_grads)
    down_grad = jnp.stack(down_grads)
    norm_grad = jnp.stack(gain_parts + shift_parts)
    embed_low = (
        math.sqrt(model_width) * jnp.concatenate([source_input_gradient, tgt_in_grad], axis=0)
    ).astype(jnp.bfloat16)
    spread_rows = lax.all_gather(embed_low, "wide", axis=0, tiled=True)
    local_ids = group_ids - offset
    inside_rows = (local_ids >= 0) & (local_ids < vocab_shard)
    embed_part = table_grad.at[jnp.clip(local_ids, 0, vocab_shard - 1)].add(
        jnp.where(inside_rows[:, None], spread_rows.astype(jnp.float32), 0.0)
    )
    attn_shard = lax.psum_scatter(attn_grad, ("dp", "wide"), scatter_dimension=1, tiled=True)
    up_shard, down_shard = (
        lax.psum_scatter(up_grad, "wide", scatter_dimension=2, tiled=True),
        lax.psum_scatter(down_grad, "wide", scatter_dimension=1, tiled=True),
    )
    up_sum, down_sum, embed_sum = lax.psum((up_shard, down_shard, embed_part), "dp")
    square_part = (
        jnp.sum(attn_shard * attn_shard)
        + (jnp.sum(up_sum * up_sum) + jnp.sum(down_sum * down_sum) + jnp.sum(embed_sum * embed_sum))
        / dp_count
    )
    square_all, norm_sum, losses = lax.psum((square_part, norm_grad, loss_own), ("dp", "wide"))
    grad_norm = jnp.sqrt(square_all + jnp.sum(norm_sum * norm_sum))
    clip_scale = clip_limit / jnp.maximum(grad_norm, clip_limit)
    attn_new, attn_m_new, attn_v_new = adamw(
        attn_master, attn_m, attn_v, clip_scale * attn_shard, rate_matrix
    )
    norm_new, norm_m_new, norm_v_new = adamw(
        norm_params, norm_m, norm_v, clip_scale * norm_sum, rate_gains
    )
    up_new, up_m_new, up_v_new = adamw(up_master, up_m, up_v, clip_scale * up_sum, rate_matrix)
    down_new, down_m_new, down_v_new = adamw(
        down_master, down_m, down_v, clip_scale * down_sum, rate_matrix
    )
    embed_new, embed_m_new, embed_v_new = adamw(
        embed_master, embed_m, embed_v, clip_scale * embed_sum, rate_matrix
    )
    ema_cols = ema_old.shape[1]
    ema_new = ema_decay * ema_old + (1.0 - ema_decay) * lax.dynamic_slice_in_dim(
        embed_new, dp_at * ema_cols, ema_cols, 1
    )
    return (
        losses,
        row_losses,
        grad_norm.reshape(1),
        attn_new,
        attn_m_new,
        attn_v_new,
        norm_new,
        norm_m_new,
        norm_v_new,
        up_new,
        up_m_new,
        up_v_new,
        down_new,
        down_m_new,
        down_v_new,
        embed_new,
        embed_m_new,
        embed_v_new,
        ema_new,
        attn_new.astype(jnp.bfloat16),
        up_new.astype(jnp.bfloat16),
        down_new.astype(jnp.bfloat16),
        embed_new.astype(jnp.bfloat16),
    )


def solution(mesh):
    in_specs = (
        P(),
        P(),
        P(),
        P(),
        P(),
        P(None, ("dp", "wide"), None),
        P(None, ("dp", "wide"), None),
        P(None, ("dp", "wide"), None),
        P(),
        P(),
        P(),
        P(None, None, "wide"),
        P(None, None, "wide"),
        P(None, None, "wide"),
        P(None, "wide", None),
        P(None, "wide", None),
        P(None, "wide", None),
        P("wide", None),
        P("wide", None),
        P("wide", None),
        P("wide", "dp"),
    )
    out_specs = (
        P(),
        P(None, ("dp", "wide"), None),
        P(),
        P(None, ("dp", "wide"), None),
        P(None, ("dp", "wide"), None),
        P(None, ("dp", "wide"), None),
        P(),
        P(),
        P(),
        P(None, None, "wide"),
        P(None, None, "wide"),
        P(None, None, "wide"),
        P(None, "wide", None),
        P(None, "wide", None),
        P(None, "wide", None),
        P("wide", None),
        P("wide", None),
        P("wide", None),
        P("wide", "dp"),
        P(None, ("dp", "wide"), None),
        P(None, None, "wide"),
        P(None, "wide", None),
        P("wide", None),
    )
    return jax.shard_map(local, mesh=mesh, in_specs=in_specs, out_specs=out_specs, check_vma=False)
```

profile of v0, /device:TPU:0, one launch (start us, length us, event | category | flops | bytes accessed | tf_op | source)
XLA Modules:
  0.0 2055.3 jit_solution(14409299491086903983)
XLA Ops:
  17.7 21.1 %gather_fusion = bf16[4096,640]{1,0:T(8,128)(2,1)} fusion(bf16[4096,640]{1,0:T(8,128)(2,1)} %convert_element_type.320, s32[4096]{0:T(1024)S(1)} %broadcast_clamp_fusion), kind=kCustom, calls=%fused_computation | custom fusion | bytes 10502144 | tf_op jit(solution)/shard_map/jit(_take)/gather | solution.py:279
  55.5 68.5 %reduce-scatter.7.cloned.1.call-done = bf16[512,640]{1,0:T(8,128)(2,1)} async-done(((bf16[4096,640]{1,0:T(8,128)(2,1)}), bf16[512,640]{1,0:T(8,128)(2,1)}) %reduce-scatter.7.cloned.1.call-update) | async-done | bytes 655376 | tf_op jit(solution)/shard_map/reduce_scatter | solution.py:282
  126.7 40.1 %all-gather.11.cloned.1.call-done = bf16[3,640,2048]{2,0,1:T(4,128)(2,1)} async-done(((bf16[3,20,2048]{2,0,1:T(4,128)(2,1)}), bf16[3,640,2048]{2,0,1:T(4,128)(2,1)}) %all-gather.11.cloned.1.call-update) | async-done | bytes 7864336 | tf_op jit(solution)/shard_map/all_gather | solution.py:260
  166.8 24.9 %fusion.160 = (bf16[1,640,2048]{2,0,1:T(2,128)(2,1)S(1)}, bf16[1,640,2048]{2,0,1:T(2,128)(2,1)S(1)}, bf16[1,640,2048]{2,0,1:T(2,128)(2,1)}) fusion(bf16[3,640,2048]{2,0,1:T(4,128)(2,1)} %all-gather.11.cloned.1.call-done), kind=kLoop, calls=%fused_computation.446 | loop fusion | bytes 15728640 | tf_op jit(solution)/shard_map/slice | solution.py:297
  218.6 26.4 %all-gather.13.cloned.1.call-done = bf16[2,640,3072]{2,1,0:T(8,128)(2,1)} async-done(((bf16[2,640,384]{2,1,0:T(8,128)(2,1)}), bf16[2,640,3072]{2,1,0:T(8,128)(2,1)}) %all-gather.13.cloned.1.call-update) | async-done | bytes 7864336 | tf_op jit(solution)/shard_map/all_gather | solution.py:262
  248.7 74.4 %all-gather.15.cloned.1.call-done = bf16[2,3072,640]{2,1,0:T(8,128)(2,1)} async-done(((bf16[2,384,640]{2,1,0:T(8,128)(2,1)}), bf16[2,3072,640]{2,1,0:T(8,128)(2,1)}) %all-gather.15.cloned.1.call-update) | async-done | bytes 7864336 | tf_op jit(solution)/shard_map/all_gather | solution.py:263
  368.8 30.3 %all-gather.19.cloned.1.call-done = bf16[2048,640]{1,0:T(8,128)(2,1)} async-done(((bf16[256,640]{1,0:T(8,128)(2,1)}), bf16[2048,640]{1,0:T(8,128)(2,1)}) %all-gather.19.cloned.1.call-update) | async-done | bytes 2621456 | tf_op jit(solution)/shard_map/all_gather | solution.py:342
  399.1 35.1 %all-gather.17.cloned.1.call-done = bf16[2048,640]{1,0:T(8,128)(2,1)} async-done(((bf16[256,640]{1,0:T(8,128)(2,1)}), bf16[2048,640]{1,0:T(8,128)(2,1)}) %all-gather.17.cloned.1.call-update) | async-done | bytes 2621456 | tf_op jit(solution)/shard_map/all_gather | solution.py:341
  439.6 117.6 %while.54 = (s32[]{:T(128)}, f32[8,512]{1,0:T(8,128)S(1)}, f32[8,512]{1,0:T(8,128)S(1)}, f32[8,512]{1,0:T(8,128)S(1)}, f32[8,512]{1,0:T(8,128)S(1)}, /*index=5*/...) while((s32[]{:T(128)}, f32[8,512]{1,0:T(8,128)S(1)}, ...), condition=%wide.region_35.36_spmd.clone, body=%wide.region_30.35_spmd.clone.sunk | while | flops 2699036672 | bytes 22741136 | solution.py:171
  439.6 9.6 fusion.270
  454.3 9.6 fusion.270
  469.0 9.6 fusion.270
  483.7 9.6 fusion.270
  498.4 9.6 fusion.270
  513.1 9.6 fusion.270
  527.8 9.6 fusion.270
  542.5 9.6 fusion.270
  557.2 14.0 all-gather
  571.3 14.0 all-gather.1
  585.4 14.0 all-gather.2
  599.5 14.0 all-gather.3
  616.0 212.4 %while.55 = (s32[]{:T(128)}, f32[4096,640]{1,0:T(8,128)}, f32[8,512,640]{2,1,0:T(8,128)}, f32[8,512]{1,0:T(8,128)S(1)}, s32[8,512]{1,0:T(8,128)S(1)}, /*index=5*...) while((s32[]{:T(128)}, f32[4096,640]{1,0:T(8,128)}, ...), condition=%wide.region_41.42_spmd.clone, body=%wide.region_40.41_spmd.clone.sunk | while | flops 8072990720 | bytes 79218912 | solution.py:201
  625.3 10.1 select_add_fusion.2
  639.9 9.2 fusion.278
  649.1 13.2 select_add_fusion.2
  666.9 9.2 fusion.278
  676.1 13.2 select_add_fusion.2
  693.8 9.2 fusion.278
  703.0 13.2 select_add_fusion.2
  720.8 9.2 fusion.278
  729.9 13.2 select_add_fusion.2
  747.7 9.2 fusion.278
  756.9 13.2 select_add_fusion.2
  774.6 9.2 fusion.278
  783.8 13.2 select_add_fusion.2
  801.6 9.2 fusion.278
  810.8 13.2 select_add_fusion.2
  838.6 57.9 %reduce-scatter.11.cloned.1.call-done = f32[256,640]{1,0:T(8,128)} async-done(((f32[2048,640]{1,0:T(8,128)}), f32[256,640]{1,0:T(8,128)}) %reduce-scatter.11.cloned.1.call-update) | async-done | bytes 655376 | tf_op jit(solution)/shard_map/reduce_scatter | solution.py:364
  898.7 58.8 %reduce-scatter.9.cloned.1.call-done = f32[256,640]{1,0:T(8,128)} async-done(((f32[2048,640]{1,0:T(8,128)}), f32[256,640]{1,0:T(8,128)}) %reduce-scatter.9.cloned.1.call-update) | async-done | bytes 655376 | tf_op jit(solution)/shard_map/reduce_scatter | solution.py:363
  1041.2 13.5 pad_maximum_fusion.1
  1072.9 12.0 pad_maximum_fusion.2
  1106.6 38.3 %scatter_custom_fusion = f32[4096,640]{1,0:T(8,128)} fusion(f32[4096,640]{1,0:T(8,128)} %get-tuple-element.420, s32[4096]{0:T(1024)} %bitcast.473, bf16[4096,640]{1,0:T(8,128)(2,1)} %all-gather.21.cloned.1.call-done, f32[]{:T(128)} %constant.228.clone.1, pred[4096]{0:T(1024)(128)(4,1)S(1)} %bitcast.479), kind=kCustom, calls=%fused_computation.42 | custom fusion | flops 7864320 | bytes 15733248 | tf_op jit(solution)/shard_map/scatter-add | solution.py:440
  1144.9 85.9 %reduce-scatter.13.cloned.1.call-done = f32[2,640,384]{2,1,0:T(8,128)} async-done(((f32[2,640,3072]{2,1,0:T(8,128)}), f32[2,640,384]{2,1,0:T(8,128)}) %reduce-scatter.13.cloned.1.call-update) | async-done | bytes 1966096 | tf_op jit(solution)/shard_map/reduce_scatter | solution.py:445
  1230.8 159.2 %reduce-scatter.15.cloned.1.call-done = f32[2,384,640]{2,1,0:T(8,128)} async-done(((f32[2,3072,640]{2,1,0:T(8,128)}), f32[2,384,640]{2,1,0:T(8,128)}) %reduce-scatter.15.cloned.1.call-update) | async-done | bytes 1966096 | tf_op jit(solution)/shard_map/reduce_scatter | solution.py:446
  1395.9 263.7 %all-reduce.6.cloned.1.call-done = f32[3,640,2048]{2,1,0:T(8,128)} async-done(((f32[3,640,2048]{2,1,0:T(8,128)}), f32[3,640,2048]{2,1,0:T(8,128)}) %all-reduce.6.cloned.1.call-update) | async-done | bytes 15728656
  1661.5 273.5 %all-reduce.8.cloned.1.call-done = (f32[2,640,384]{2,1,0:T(8,128)}, f32[2,384,640]{2,1,0:T(8,128)}, f32[4096,640]{1,0:T(8,128)}) async-done(((f32[2,640,384]{2,1,0:T(8,128)}, f32[2,384,640]{2,1,0:T(8,128)}, f32[4096,640]{1,0:T(8,128)}), (f32[2,640,384]{2,1,0:T(8,128)}, f32[2,384,640]{2,1,0:T(8,128)}, f32[4096,640]{1,0:T(8,128)})) %all-reduce.8.cloned.1.call-update) | async-done | bytes 14417936 | tf_op jit(solution)/shard_map/psum | solution.py:448
  1949.4 40.0 %all-reduce.1 = (f32[2]{0:T(128)}, f32[]{:T(128)}, f32[14,640]{1,0:T(8,128)S(1)}) all-reduce(f32[2]{0:T(128)S(1)} %dynamic-slice_reduce_fusion, f32[]{:T(128)S(6)} %add.693, f32[14,640]{1,0:T(8,128)S(1)} %stack.78), channel_id=1, replica_groups=mesh['dp'=4,'wide'=8] {'dp','wide'}, use_global_device_ids=true, to_apply=%region_39.40 | all-reduce | flops 8963 | bytes 71704 | tf_op jit(solution)/shard_map/psum | solution.py:454
  1991.4 28.8 %fusion.145 = (bf16[4096,640]{1,0:T(8,128)(2,1)}, f32[4096,640]{1,0:T(8,128)}, f32[4096,640]{1,0:T(8,128)}, f32[4096,640]{1,0:T(8,128)}) fusion(f32[4096,640]{1,0:T(8,128)} %param.44, f32[4096,640]{1,0:T(8,128)} %get-tuple-element.706, f32[]{:T(128)S(6)} %div.250, f32[4096,640]{1,0:T(8,128)} %param.46, f32[4096,640]{1,0:T(8,128)} %param.45), kind=kLoop, calls=%fused_computation.438 | loop fusion | flops 39321600 | bytes 78643200 | tf_op jit(solution)/shard_map/convert_element_type | solution.py:497
  (1043 shorter events, 378.1 us)
Async XLA Ops:
  8.0 115.9 %reduce-scatter.7.cloned.1.call-start = ((), (), s32[]{:S(2)}) async-start(), calls=%async_computation.5 | async-start | bytes 5898240 | tf_op jit(solution)/shard_map/reduce_scatter | solution.py:282
  44.8 122.0 %all-gather.11.cloned.1.call-start = ((), (), s32[]{:S(2)}) async-start(), calls=%async_computation.6 | async-start | bytes 10813440 | tf_op jit(solution)/shard_map/all_gather | solution.py:260
  46.8 198.1 %all-gather.13.cloned.1.call-start = ((), (), s32[]{:S(2)}) async-start(), calls=%async_computation.7 | async-start | bytes 8847360 | tf_op jit(solution)/shard_map/all_gather | solution.py:262
  47.9 275.2 %all-gather.15.cloned.1.call-start = ((), (), s32[]{:S(2)}) async-start(), calls=%async_computation.8 | async-start | bytes 8847360 | tf_op jit(solution)/shard_map/all_gather | solution.py:263
  50.6 348.5 %all-gather.19.cloned.1.call-start = ((), (), s32[]{:S(2)}) async-start(), calls=%async_computation.10 | async-start | bytes 2949120 | tf_op jit(solution)/shard_map/all_gather | solution.py:342
  50.7 74.8 %copy-start.235 = (pred[256]{0:T(512)(128)(4,1)}, pred[256]{0:T(512)(128)(4,1)S(1)}, u32[]{:S(2)}) copy-start(pred[256]{0:T(512)(128)(4,1)S(1)} %compare_reduce_fusion) | copy-start | bytes 772
  52.0 293.7 %copy-start.154 = (pred[3072]{0:T(1024)(128)(4,1)}, pred[3072]{0:T(1024)(128)(4,1)S(1)}, u32[]{:S(2)}) copy-start(pred[3072]{0:T(1024)(128)(4,1)S(1)} %iota_compare_fusion.2) | copy-start | bytes 9220
  53.9 72.1 %copy-start.189 = (f32[640]{0:T(1024)}, f32[640]{0:T(1024)S(1)}, u32[]{:S(2)}) copy-start(f32[640]{0:T(1024)S(1)} %get-tuple-element.645) | copy-start | bytes 7684
  53.9 72.6 %copy-start.187 = (f32[640]{0:T(1024)}, f32[640]{0:T(1024)S(1)}, u32[]{:S(2)}) copy-start(f32[640]{0:T(1024)S(1)} %get-tuple-element.643) | copy-start | bytes 7684
  53.9 191.0 %copy-start.152 = (f32[640]{0:T(1024)}, f32[640]{0:T(1024)S(1)}, u32[]{:S(2)}) copy-start(f32[640]{0:T(1024)S(1)} %get-tuple-element.641) | copy-start | bytes 7684
  53.9 191.0 %copy-start.156 = (f32[640]{0:T(1024)}, f32[640]{0:T(1024)S(1)}, u32[]{:S(2)}) copy-start(f32[640]{0:T(1024)S(1)} %get-tuple-element.640) | copy-start | bytes 7684
  53.9 277.5 %copy-start.177 = (f32[640]{0:T(1024)}, f32[640]{0:T(1024)S(1)}, u32[]{:S(2)}) copy-start(f32[640]{0:T(1024)S(1)} %get-tuple-element.637) | copy-start | bytes 7684
  53.9 299.6 %copy-start.175 = (f32[640]{0:T(1024)}, f32[640]{0:T(1024)S(1)}, u32[]{:S(2)}) copy-start(f32[640]{0:T(1024)S(1)} %get-tuple-element.639) | copy-start | bytes 7684
  53.9 299.6 %copy-start.185 = (f32[640]{0:T(1024)}, f32[640]{0:T(1024)S(1)}, u32[]{:S(2)}) copy-start(f32[640]{0:T(1024)S(1)} %get-tuple-element.638) | copy-start | bytes 7684
  53.9 306.5 %copy-start.146 = (f32[640]{0:T(1024)}, f32[640]{0:T(1024)S(1)}, u32[]{:S(2)}) copy-start(f32[640]{0:T(1024)S(1)} %get-tuple-element.635) | copy-start | bytes 7684
  53.9 306.5 %copy-start.150 = (f32[640]{0:T(1024)}, f32[640]{0:T(1024)S(1)}, u32[]{:S(2)}) copy-start(f32[640]{0:T(1024)S(1)} %get-tuple-element.634) | copy-start | bytes 7684
  53.9 310.9 %copy-start.164 = (f32[640]{0:T(1024)}, f32[640]{0:T(1024)S(1)}, u32[]{:S(2)}) copy-start(f32[640]{0:T(1024)S(1)} %get-tuple-element.633) | copy-start | bytes 7684
  125.5 86.2 %copy-start.24 = (f32[256,640]{1,0:T(8,128)}, f32[256,640]{1,0:T(8,128)S(1)}, u32[]{:S(2)}) copy-start(f32[256,640]{1,0:T(8,128)S(1)} %get-tuple-element.731) | copy-start | bytes 1966084
  125.5 90.6 %copy-start.26 = (f32[256,640]{1,0:T(8,128)}, f32[256,640]{1,0:T(8,128)S(1)}, u32[]{:S(2)}) copy-start(f32[256,640]{1,0:T(8,128)S(1)} %get-tuple-element.748) | copy-start | bytes 1966084
  125.7 66.0 %copy-start.218 = (f32[256]{0:T(256)}, f32[256]{0:T(256)S(1)}, u32[]{:S(2)}) copy-start(f32[256]{0:T(256)S(1)} %broadcast_multiply_fusion.28) | copy-start | bytes 3076
  126.0 65.7 %copy-start.239 = (f32[256]{0:T(256)}, f32[256]{0:T(256)S(1)}, u32[]{:S(2)}) copy-start(f32[256]{0:T(256)S(1)} %add_rsqrt_fusion.9) | copy-start | bytes 3076
  126.0 65.7 %copy-start.237 = (f32[256]{0:T(256)}, f32[256]{0:T(256)S(1)}, u32[]{:S(2)}) copy-start(f32[256]{0:T(256)S(1)} %add_rsqrt_fusion.8) | copy-start | bytes 3076
  126.2 72.6 %copy-start.75 = (bf16[256,640]{1,0:T(8,128)(2,1)}, bf16[256,640]{1,0:T(8,128)(2,1)S(1)}, u32[]{:S(2)}) copy-start(bf16[256,640]{1,0:T(8,128)(2,1)S(1)} %add_convert_fusion.9) | copy-start | bytes 983044
  126.7 80.6 %copy-start.73 = (bf16[256,640]{1,0:T(8,128)(2,1)}, bf16[256,640]{1,0:T(8,128)(2,1)S(1)}, u32[]{:S(2)}) copy-start(bf16[256,640]{1,0:T(8,128)(2,1)S(1)} %add_convert_fusion.8) | copy-start | bytes 983044
  213.4 31.5 %copy-start.183 = (f32[256]{0:T(256)}, f32[256]{0:T(256)S(1)}, u32[]{:S(2)}) copy-start(f32[256]{0:T(256)S(1)} %broadcast_multiply_fusion.27) | copy-start | bytes 3076
  215.1 29.8 %copy-start.204 = (f32[256]{0:T(256)}, f32[256]{0:T(256)S(1)}, u32[]{:S(2)}) copy-start(f32[256]{0:T(256)S(1)} %add_rsqrt_fusion.7) | copy-start | bytes 3076
  216.1 28.8 %copy-start.132 = (bf16[8,64,256]{2,1,0:T(8,128)(2,1)}, bf16[8,64,256]{2,1,0:T(8,128)(2,1)S(1)}, u32[]{:S(2)}) copy-start(bf16[8,64,256]{2,1,0:T(8,128)(2,1)S(1)} %convolution_convert_fusion.11) | copy-start | bytes 786436
  248.7 102.1 %copy-start.3 = (f32[256,3072]{1,0:T(8,128)}, f32[256,3072]{1,0:T(8,128)S(1)}, u32[]{:S(2)}) copy-start(f32[256,3072]{1,0:T(8,128)S(1)} %fusion.29) | copy-start | bytes 9437188
  366.5 67.7 %all-gather.17.cloned.1.call-start = ((), (), s32[]{:S(2)}) async-start(), calls=%async_computation.9 | async-start | bytes 2949120 | tf_op jit(solution)/shard_map/all_gather | solution.py:341
  367.3 529.2 %reduce-scatter.11.cloned.1.call-start = ((), (), s32[]{:S(2)}) async-start(), calls=%async_computation.12 | async-start | bytes 5898240 | tf_op jit(solution)/shard_map/reduce_scatter | solution.py:364
  368.0 246.8 %copy-start.158 = (f32[1,16,2,128]{3,1,2,0:T(8,128)}, f32[1,16,2,128]{3,1,2,0:T(8,128)S(1)}, u32[]{:S(2)}) copy-start(f32[1,16,2,128]{3,1,2,0:T(8,128)S(1)} %copy.361) | copy-start | bytes 49156
  666.9 22.4 %slice-start = ((s8[5242880]{0:T(1024)(128)(4,1)}), s8[1048576]{0:T(1024)(128)(4,1)S(1)}, s32[]{:S(2)}) async-start(s8[5242880]{0:T(1024)(128)(4,1)} %bitcast.358), calls=%async_computation.18 | async-start | bytes 2097152 | tf_op jit(solution)/shard_map/while
  693.8 22.4 %slice-start = ((s8[5242880]{0:T(1024)(128)(4,1)}), s8[1048576]{0:T(1024)(128)(4,1)S(1)}, s32[]{:S(2)}) async-start(s8[5242880]{0:T(1024)(128)(4,1)} %bitcast.358), calls=%async_computation.18 | async-start | bytes 2097152 | tf_op jit(solution)/shard_map/while
  720.7 22.4 %slice-start = ((s8[5242880]{0:T(1024)(128)(4,1)}), s8[1048576]{0:T(1024)(128)(4,1)S(1)}, s32[]{:S(2)}) async-start(s8[5242880]{0:T(1024)(128)(4,1)} %bitcast.358), calls=%async_computation.18 | async-start | bytes 2097152 | tf_op jit(solution)/shard_map/while
  747.7 22.4 %slice-start = ((s8[5242880]{0:T(1024)(128)(4,1)}), s8[1048576]{0:T(1024)(128)(4,1)S(1)}, s32[]{:S(2)}) async-start(s8[5242880]{0:T(1024)(128)(4,1)} %bitcast.358), calls=%async_computation.18 | async-start | bytes 2097152 | tf_op jit(solution)/shard_map/while
  774.6 22.4 %slice-start = ((s8[5242880]{0:T(1024)(128)(4,1)}), s8[1048576]{0:T(1024)(128)(4,1)S(1)}, s32[]{:S(2)}) async-start(s8[5242880]{0:T(1024)(128)(4,1)} %bitcast.358), calls=%async_computation.18 | async-start | bytes 2097152 | tf_op jit(solution)/shard_map/while
  837.4 120.1 %reduce-scatter.9.cloned.1.call-start = ((), (), s32[]{:S(2)}) async-start(), calls=%async_computation.11 | async-start | bytes 5898240 | tf_op jit(solution)/shard_map/reduce_scatter | solution.py:363
  837.5 59.0 %copy-start.165 = (f32[640]{0:T(1024)S(1)}, f32[640]{0:T(1024)}, u32[]{:S(2)}) copy-start(f32[640]{0:T(1024)} %copy-done.164) | copy-start | bytes 7684
  837.5 59.0 %copy-start.211 = (f32[256]{0:T(256)S(1)}, f32[256]{0:T(256)}, u32[]{:S(2)}) copy-start(f32[256]{0:T(256)} %copy-done.210) | copy-start | bytes 3076
  837.5 59.0 %copy-start.225 = (f32[256]{0:T(256)S(1)}, f32[256]{0:T(256)}, u32[]{:S(2)}) copy-start(f32[256]{0:T(256)} %copy-done.224) | copy-start | bytes 3076
  837.5 120.0 %copy-start.207 = (f32[256]{0:T(256)S(1)}, f32[256]{0:T(256)}, u32[]{:S(2)}) copy-start(f32[256]{0:T(256)} %copy-done.206) | copy-start | bytes 3076
  837.6 120.0 %copy-start.217 = (f32[256]{0:T(256)S(1)}, f32[256]{0:T(256)}, u32[]{:S(2)}) copy-start(f32[256]{0:T(256)} %copy-done.216) | copy-start | bytes 3076
  838.0 122.4 %copy-start.36 = (f32[256,3072]{1,0:T(8,128)S(1)}, f32[256,3072]{1,0:T(8,128)}, u32[]{:S(2)}) copy-start(f32[256,3072]{1,0:T(8,128)} %copy-done.35) | copy-start | bytes 9437188
  838.0 268.1 %all-gather.21.cloned.1.call-start = ((), (), s32[]{:S(2)}) async-start(), calls=%async_computation.15 | async-start | bytes 5898240 | tf_op jit(solution)/shard_map/all_gather | solution.py:437
  1028.2 202.6 %reduce-scatter.13.cloned.1.call-start = ((), (), s32[]{:S(2)}) async-start(), calls=%async_computation.13 | async-start | bytes 17694720 | tf_op jit(solution)/shard_map/reduce_scatter | solution.py:445
  1054.8 335.3 %reduce-scatter.15.cloned.1.call-start = ((), (), s32[]{:S(2)}) async-start(), calls=%async_computation.14 | async-start | bytes 17694720 | tf_op jit(solution)/shard_map/reduce_scatter | solution.py:446
  1084.9 574.7 %all-reduce.6.cloned.1.call-start = ((), (), s32[]{:S(2)}) async-start(), calls=%async_computation.16 | async-start | bytes 31457280
  1106.0 829.0 %all-reduce.8.cloned.1.call-start = ((), (), s32[]{:S(2)}) async-start(), calls=%async_computation.17 | async-start | bytes 28835840 | tf_op jit(solution)/shard_map/psum | solution.py:448
  (263 other events, 1105.9 us)
Sparse Core Ops, SparseCore 0:
  44.9 78.9 reduce-scatter.6
  366.6 32.4 all-gather.18
  401.3 32.8 all-gather.16
  837.5 58.9 reduce-scatter.10
  899.2 58.2 reduce-scatter.8
  1028.3 75.5 all-gather.20
Sparse Core Ops, SparseCore 1:
  48.7 118.0 all-gather.10
  168.8 76.0 all-gather.12
  247.0 76.1 all-gather.14
  1054.8 175.9 reduce-scatter.12
  1233.1 156.8 reduce-scatter.14
  1396.3 263.3 all-reduce.5
  1664.6 270.4 all-reduce.7
where the time goes:
time: 2060 us
  waiting for transfers between devices  1180 us (57%)
  matrix products  421 us (20%)
  other arithmetic  221 us (11%)
  local copies, waits for them, and re-layouts  113 us (5%)
  blocking collectives  95.9 us (5%)
  between operations  25.7 us (1%)
    psum x1, waiting for transfers between devices, local(): lax.psum((up_shard, down_shard, embed_part), 'dp')  273 us
    unnamed x14, waiting for transfers between devices  265 us
    dot_general x35, matrix products, dot_rows(): lax.dot_general(left, right, (((1,), (1,)), ((), ())), preferred_element_...  187 us
    reduce_scatter x1, waiting for transfers between devices, local(): lax.psum_scatter(down_grad, 'wide', scatter_dimension=1, tiled=True)  159 us
    dot_general x27, matrix products, dot_cols(): lax.dot_general(left, right, (((0,), (0,)), ((), ())), preferred_element_...  141 us
    reduce_scatter x1, waiting for transfers between devices, local(): lax.psum_scatter(up_grad, 'wide', scatter_dimension=2, tiled=True)  85.9 us
    all_gather x1, waiting for transfers between devices, local(): lax.all_gather(down_master.astype(jnp.bfloat16), 'wide', axis=1, tiled=True)  74.4 us
    reduce_scatter x1, waiting for transfers between devices, local(): lax.psum_scatter(jnp.where(inside[:, None], found_rows, 0.0).astype(jnp.b...  68.5 us
  transfers between devices with their start and end apart: 13, of which 12 were waited for; matrix products, arithmetic and copies ran while one was open for 9% of the time, Pallas kernels for 0%

commit v1 on v0

--- a/solution.py
+++ b/solution.py
@@ -1,8 +1,13 @@
 import math
+
+import functools
 
 import jax
 import jax.numpy as jnp
+import numpy as np
 from jax import lax
+from jax.experimental import pallas as pl
+from jax.experimental.pallas import tpu as pltpu
 from jax.sharding import PartitionSpec as P
 
 HEADS = 8
@@ -23,15 +28,11 @@
 norm_count = 7
 
 
-def merged(part, axis, combine):
-    gathered = jax.tree.map(lambda a: lax.all_gather(a, axis), part)
-
-    def take(source):
-        return jax.tree.map(lambda a: lax.dynamic_index_in_dim(a, source, 0, False), gathered)
-
-    return lax.fori_loop(
-        1, lax.axis_size(axis), lambda source, state: combine(state, take(source)), take(0)
-    )
+def merged(part, axis):
+    gathered = lax.all_gather(jnp.stack(part), axis)
+    row_peak = jnp.max(gathered[:, 0], axis=0)
+    row_total = jnp.sum(gathered[:, 1] * jnp.exp(gathered[:, 0] - row_peak), axis=0)
+    return row_peak, row_total, jnp.sum(gathered[:, 2], axis=0), jnp.sum(gathered[:, 3], axis=0)
 
 
 def dot_rows(left, right):
@@ -47,10 +48,10 @@
 
 
 def sinusoid(length, model_width):
-    places = jnp.arange(length, dtype=jnp.float32)[:, None]
-    halves = jnp.arange(model_width // 2, dtype=jnp.float32)[None, :]
-    angles = places * jnp.exp(halves * (-2.0 * math.log(10000.0) / model_width))
-    return jnp.concatenate([jnp.sin(angles), jnp.cos(angles)], axis=1)
+    places = np.arange(length, dtype=np.float64)[:, None]
+    halves = np.arange(model_width // 2, dtype=np.float64)[None, :]
+    angles = places * np.exp(halves * (-2.0 * math.log(10000.0) / model_width))
+    return jnp.asarray(np.concatenate([np.sin(angles), np.cos(angles)], axis=1), jnp.float32)
 
 
 def layer_norm(values, gain, shift):
@@ -136,9 +137,7 @@
     pair_low = jnp.concatenate(
         [key_grad.reshape(tokens, width), value_grad.reshape(tokens, width)], axis=1
     ).astype(jnp.bfloat16)
-    block_grad = jnp.concatenate(
-        [dot_cols(q_in, query_low), dot_cols(kv_in, pair_low), out_weight_grad], axis=1
-    )
+    block_grad = (dot_cols(q_in, query_low), dot_cols(kv_in, pair_low), out_weight_grad)
     return (
         dot_rows(query_low, block[:, :width]),
         dot_rows(pair_low, block[:, width : 3 * width]),
@@ -147,69 +146,132 @@
 
 
 def ffn_pass(hidden, inner, down, width_now):
+    inner = inner[:, : down.shape[0]]
     units = jnp.arange(inner.shape[1])[None, :]
     active = (units < width_now) & (inner > 0)
     act_low = jnp.where(active, inner, 0.0).astype(jnp.bfloat16)
     return (hidden + jnp.dot(act_low, down, preferred_element_type=jnp.float32), active, act_low)
 
 
+def head_stats_kernel(block, offset_ref, table_ref, z_ref, target_ref, exp_ref, stat_ref):
+    tile, rows = exp_ref.shape
+    first = offset_ref[0] + pl.program_id(0) * tile
+    ids = first + lax.broadcasted_iota(jnp.int32, (tile, block), 0)
+
+    def step(index, carry):
+        at = pl.ds(pl.multiple_of(index * block, block), block)
+        logits = dot_rows(table_ref[...], z_ref[at, :])
+        peak = jnp.max(logits, axis=0, keepdims=True)
+        grown = jnp.exp(logits - peak)
+        exp_ref[:, at] = grown.astype(jnp.bfloat16)
+        hits = ids == target_ref[:, at]
+        stat_ref[0, 0:1, at] = peak
+        stat_ref[0, 1:2, at] = jnp.sum(grown, axis=0, keepdims=True)
+        stat_ref[0, 2:3, at] = jnp.sum(jnp.where(hits, logits, 0.0), axis=0, keepdims=True)
+        stat_ref[0, 3:4, at] = jnp.sum(logits, axis=0, keepdims=True)
+        return carry
+
+    lax.fori_loop(0, rows // block, step, 0, unroll=4)
+
+
 def head_stats(head_in, row_targets, table_part, offset):
-    row_count = head_in.shape[0]
-    block_rows = math.gcd(row_count, 512)
-    columns = offset + jnp.arange(table_part.shape[0])
-
-    def one_block(block_items):
-        rows_low, block_targets = block_items
-        logits = dot_rows(rows_low, table_part)
-        row_peak = jnp.max(logits, axis=-1)
-        row_total = jnp.sum(jnp.exp(logits - row_peak[:, None]), axis=-1)
-        target_logit = jnp.sum(
-            jnp.where(columns[None, :] == block_targets[:, None], logits, 0.0), axis=-1
-        )
-        return (row_peak, row_total, target_logit, jnp.sum(logits, axis=-1))
-
-    results = lax.map(
-        one_block,
-        (head_in.reshape(-1, block_rows, head_in.shape[1]), row_targets.reshape(-1, block_rows)),
-    )
-    return tuple((stat_part.reshape(-1) for stat_part in results))
-
-
-def head_grads(head_in, row_targets, row_weights, log_total, table_part, offset):
-    row_count, model_width = head_in.shape
-    block_rows = math.gcd(row_count, 512)
-    columns = offset + jnp.arange(table_part.shape[0])
-
-    def one_block(table_grad, block_items):
-        rows_low, block_targets, block_weights, block_lse = block_items
-        probs = jnp.exp(dot_rows(rows_low, table_part) - block_lse[:, None])
-        hits = columns[None, :] == block_targets[:, None]
-        logit_low = (
-            block_weights[:, None] * (jnp.where(hits, probs - (1.0 - smooth), probs) - smooth / V)
-        ).astype(jnp.bfloat16)
-        return (
-            table_grad + dot_cols(logit_low, rows_low),
-            jnp.dot(logit_low, table_part, preferred_element_type=jnp.float32),
-        )
-
-    block_items = (
-        head_in.reshape(-1, block_rows, model_width),
-        row_targets.reshape(-1, block_rows),
-        row_weights.reshape(-1, block_rows),
-        log_total.reshape(-1, block_rows),
-    )
-    table_grad, row_grads = lax.scan(
-        one_block, jnp.zeros(table_part.shape, jnp.float32), block_items
-    )
-    return (row_grads.reshape(row_count, model_width), table_grad)
-
-
-def join_stats(first_part, second_part):
-    row_peak = jnp.maximum(first_part[0], second_part[0])
-    row_total = first_part[1] * jnp.exp(first_part[0] - row_peak) + second_part[1] * jnp.exp(
-        second_part[0] - row_peak
-    )
-    return (row_peak, row_total, first_part[2] + second_part[2], first_part[3] + second_part[3])
+    rows, width = head_in.shape
+    vocab = table_part.shape[0]
+    tile, block = math.gcd(vocab, 512), math.gcd(rows, 512)
+    tiles = vocab // tile
+    exps, stats = pl.pallas_call(
+        functools.partial(head_stats_kernel, block),
+        out_shape=(
+            jax.ShapeDtypeStruct((vocab, rows), jnp.bfloat16),
+            jax.ShapeDtypeStruct((tiles, 4, rows), jnp.float32),
+        ),
+        grid_spec=pltpu.PrefetchScalarGridSpec(
+            num_scalar_prefetch=1,
+            grid=(tiles,),
+            in_specs=[
+                pl.BlockSpec((tile, width), lambda t, o: (t, 0)),
+                pl.BlockSpec((rows, width), lambda t, o: (0, 0), pipeline_mode=pl.Buffered(1)),
+                pl.BlockSpec((1, rows), lambda t, o: (0, 0)),
+            ],
+            out_specs=(
+                pl.BlockSpec((tile, rows), lambda t, o: (t, 0)),
+                pl.BlockSpec((1, 4, rows), lambda t, o: (t, 0, 0)),
+            ),
+        ),
+        compiler_params=pltpu.CompilerParams(vmem_limit_bytes=56 << 20),
+        name="head_stats",
+    )(offset.reshape(1), table_part, head_in, row_targets.reshape(1, rows))
+    return exps, stats
+
+
+def head_grads_kernel(
+    block, offset_ref, exp_ref, table_t_ref, z_ref, target_ref, weight_ref, scale_ref, dz_ref,
+    dtable_ref, acc_ref,
+):
+    tile, rows = exp_ref.shape
+    t = pl.program_id(0)
+    last = pl.num_programs(0) - 1
+    first = offset_ref[0] + t * tile
+    ids = first + lax.broadcasted_iota(jnp.int32, (tile, block), 0)
+
+    def step(index, carry):
+        at = pl.ds(pl.multiple_of(index * block, block), block)
+        weight = weight_ref[:, at]
+        hits = ids == target_ref[:, at]
+        grad = exp_ref[:, at].astype(jnp.float32) * scale_ref[0, :, at] - jnp.where(
+            hits, weight * (1.0 - smooth + smooth / V), weight * (smooth / V)
+        )
+        low = grad.astype(jnp.bfloat16)
+        part = jnp.dot(low, z_ref[at, :], preferred_element_type=jnp.float32)
+        dtable_ref[...] = jnp.where(index == 0, part, dtable_ref[...] + part)
+        back = jnp.dot(table_t_ref[...], low, preferred_element_type=jnp.float32)
+        total = jnp.where(t == 0, back, acc_ref[index] + back)
+        acc_ref[index] = total
+
+        @pl.when(t == last)
+        def _():
+            dz_ref[at, :] = total.T.astype(jnp.bfloat16)
+
+        return carry
+
+    lax.fori_loop(0, rows // block, step, 0)
+
+
+def head_grads(head_in, row_targets, row_weights, scale, exps, table_t, offset):
+    rows, width = head_in.shape
+    vocab = exps.shape[0]
+    tile, block = math.gcd(vocab, 512), math.gcd(rows, 1024)
+    tiles = vocab // tile
+    row = pl.BlockSpec((1, rows), lambda t, o: (0, 0))
+    return pl.pallas_call(
+        functools.partial(head_grads_kernel, block),
+        out_shape=(
+            jax.ShapeDtypeStruct((rows, width), jnp.bfloat16),
+            jax.ShapeDtypeStruct((vocab, width), jnp.float32),
+        ),
+        grid_spec=pltpu.PrefetchScalarGridSpec(
+            num_scalar_prefetch=1,
+            grid=(tiles,),
+            in_specs=[
+                pl.BlockSpec((tile, rows), lambda t, o: (t, 0)),
+                pl.BlockSpec((width, tile), lambda t, o: (0, t)),
+                pl.BlockSpec((rows, width), lambda t, o: (0, 0), pipeline_mode=pl.Buffered(1)),
+                row,
+                row,
+                pl.BlockSpec((1, 1, rows), lambda t, o: (t, 0, 0)),
+            ],
+            out_specs=(
+                pl.BlockSpec((rows, width), lambda t, o: (0, 0), pipeline_mode=pl.Buffered(1)),
+                pl.BlockSpec((tile, width), lambda t, o: (t, 0)),
+            ),
+            scratch_shapes=[pltpu.VMEM((rows // block, width, block), jnp.float32)],
+        ),
+        compiler_params=pltpu.CompilerParams(vmem_limit_bytes=60 << 20),
+        name="head_grads",
+    )(
+        offset.reshape(1), exps, table_t, head_in, row_targets.reshape(1, rows),
+        row_weights.reshape(1, rows), scale,
+    )
 
 
 def adamw(weight, first_m, second_m, grad_item, step_rate):
@@ -307,9 +369,11 @@
     cross_low = cross_val.astype(jnp.bfloat16)
     passes = []
     final_list = []
+    pass_units = (up_full.shape[2], up_full.shape[2] // 2)
     for pass_index in range(2):
+        held = pass_units[pass_index]
         enc_out, enc_active, enc_act = ffn_pass(
-            src_hidden, src_inner, down_full[0], pass_widths[pass_index]
+            src_hidden, src_inner, down_full[0, :held], pass_widths[pass_index]
         )
         mem_val, mem_stats = norm_at(enc_out, 2)
         mem_low = mem_val.astype(jnp.bfloat16)
@@ -317,9 +381,9 @@
         crossed = tgt_hidden + x_att
         dff_val, dff_stats = norm_at(crossed, 5)
         dff_low = dff_val.astype(jnp.bfloat16)
-        dec_inner = jnp.dot(dff_low, up_full[1], preferred_element_type=jnp.float32)
+        dec_inner = jnp.dot(dff_low, up_full[1, :, :held], preferred_element_type=jnp.float32)
         dec_out, dec_active, dec_act = ffn_pass(
-            crossed, dec_inner, down_full[1], pass_widths[pass_index]
+            crossed, dec_inner, down_full[1, :held], pass_widths[pass_index]
         )
         fin_val, fin_stats = norm_at(dec_out, 6)
         passes.append(
@@ -346,22 +410,44 @@
     row_masks = jnp.tile(
         rows_of(pad_mask, group_start, wide_count * seq_dev).astype(jnp.float32), 2
     )
-    row_stats = head_stats(head_in, row_targets, table_local, offset)
-    row_peak, row_total, target_logit, logit_sum = merged(row_stats, "wide", join_stats)
+    chunk = math.gcd(head_in.shape[0], 4096)
+    chunks = [slice(at, at + chunk) for at in range(0, head_in.shape[0], chunk)]
+    exps, stats = zip(
+        *[head_stats(head_in[at], row_targets[at], table_local, offset) for at in chunks]
+    )
+    stats = jnp.concatenate(stats, axis=2)
+    tile_peaks = stats[:, 0]
+    own_peak = jnp.max(tile_peaks, axis=0)
+    own_total = jnp.sum(stats[:, 1] * jnp.exp(tile_peaks - own_peak), axis=0)
+    row_peak, row_total, target_logit, logit_sum = merged(
+        (own_peak, own_total, jnp.sum(stats[:, 2], axis=0), jnp.sum(stats[:, 3], axis=0)), "wide"
+    )
     row_weights = row_masks / count_all
     log_total = row_peak + jnp.log(row_total)
     row_error = log_total - (1.0 - smooth) * target_logit - smooth / V * logit_sum
     row_loss = (row_weights * row_error).reshape(2, -1)
     row_plain = (row_masks * row_error).reshape(2, -1)
-    row_grads, table_grad = head_grads(
-        head_in, row_targets, row_weights, log_total, table_local, offset
-    )
+    scale = (row_weights * jnp.exp(tile_peaks - log_total))[:, None, :]
+    row_grads, table_grad = zip(
+        *[
+            head_grads(
+                head_in[at], row_targets[at], row_weights[at], scale[:, :, at], part,
+                table_local.T, offset,
+            )
+            for at, part in zip(chunks, exps)
+        ]
+    )
+    row_grads, table_grad = jnp.concatenate(row_grads), sum(table_grad)
     half_rows = head_in.shape[0] // 2
     loss_own = jnp.sum(lax.dynamic_slice_in_dim(row_loss, wide_at * tokens, tokens, 1), axis=1)
     plain_own = lax.dynamic_slice_in_dim(row_plain, wide_at * tokens, tokens, 1)
     final_grads = (
-        lax.psum_scatter(row_grads[:half_rows], "wide", scatter_dimension=0, tiled=True),
-        lax.psum_scatter(row_grads[half_rows:], "wide", scatter_dimension=0, tiled=True),
+        lax.psum_scatter(
+            row_grads[:half_rows], "wide", scatter_dimension=0, tiled=True
+        ).astype(jnp.float32),
+        lax.psum_scatter(
+            row_grads[half_rows:], "wide", scatter_dimension=0, tiled=True
+        ).astype(jnp.float32),
     )
     row_losses = plain_own.reshape(2, seq_dev, length)
     gain_parts = [jnp.zeros((model_width,), jnp.float32) for index in range(norm_count)]
@@ -377,9 +463,9 @@
     source_hidden_gradient = jnp.zeros((tokens, model_width), jnp.float32)
     tgt_hidden_grad = jnp.zeros((tokens, model_width), jnp.float32)
     cross_grad = jnp.zeros((tokens, model_width), jnp.float32)
-    cross_weight = jnp.zeros(attn_full.shape[1:], jnp.float32)
-    up_grads = [jnp.zeros(up_full.shape[1:], jnp.float32) for index in range(2)]
-    down_grads = [jnp.zeros(down_full.shape[1:], jnp.float32) for index in range(2)]
+    cross_weight = []
+    up_grads = [[], []]
+    down_grads = [[], []]
     for pass_index in range(2):
         (
             enc_active,
@@ -394,26 +480,32 @@
         ) = passes[pass_index]
         out_grad = backward_layer_norm(final_grads[pass_index], fin_stats, 6)
         out_low = out_grad.astype(jnp.bfloat16)
-        down_grads[1] = down_grads[1] + dot_cols(dec_act, out_low)
-        dec_low = jnp.where(dec_active, dot_rows(out_low, down_full[1]), 0.0).astype(jnp.bfloat16)
-        up_grads[1] = up_grads[1] + dot_cols(dff_low, dec_low)
-        crossed_grad = out_grad + backward_layer_norm(dot_rows(dec_low, up_full[1]), dff_stats, 5)
+        held = pass_units[pass_index]
+        down_grads[1].append(dot_cols(dec_act, out_low))
+        dec_low = jnp.where(
+            dec_active, dot_rows(out_low, down_full[1, :held]), 0.0
+        ).astype(jnp.bfloat16)
+        up_grads[1].append(dot_cols(dec_low, dff_low))
+        crossed_grad = out_grad + backward_layer_norm(
+            dot_rows(dec_low, up_full[1, :, :held]), dff_stats, 5
+        )
         query_in, memory_in, block_grad = attention_backward_pass(
             x_kept, crossed_grad.astype(jnp.bfloat16), attn_full[2]
         )
-        cross_weight = cross_weight + block_grad
+        cross_weight.append(block_grad)
         tgt_hidden_grad = tgt_hidden_grad + crossed_grad
         cross_grad = cross_grad + query_in
         enc_grad = backward_layer_norm(memory_in, mem_stats, 2)
         enc_low = enc_grad.astype(jnp.bfloat16)
-        down_grads[0] = down_grads[0] + dot_cols(enc_act, enc_low)
-        src_inner_grad = src_inner_grad + jnp.where(
-            enc_active, dot_rows(enc_low, down_full[0]), 0.0
+        down_grads[0].append(dot_cols(enc_act, enc_low))
+        src_inner_grad = src_inner_grad + jnp.pad(
+            jnp.where(enc_active, dot_rows(enc_low, down_full[0, :held]), 0.0),
+            ((0, 0), (0, src_inner.shape[1] - held)),
         )
         source_hidden_gradient = source_hidden_gradient + enc_grad
     tgt_hidden_grad = tgt_hidden_grad + backward_layer_norm(cross_grad, cross_stats, 4)
     src_inner_low = src_inner_grad.astype(jnp.bfloat16)
-    up_grads[0] = dot_cols(sff_low, src_inner_low)
+    up_grads[0].append(dot_cols(src_inner_low, sff_low))
     source_hidden_gradient = source_hidden_gradient + backward_layer_norm(
         dot_rows(src_inner_low, up_full[0]), sff_stats, 1
     )
@@ -427,9 +519,30 @@
     source_input_gradient = source_hidden_gradient + backward_layer_norm(
         source_query_input + source_key_value_input, source_norm_statistics, 0
     )
-    attn_grad = jnp.stack([source_norm_weight, tgt_weight, cross_weight])
-    up_grad = jnp.stack(up_grads)
-    down_grad = jnp.stack(down_grads)
+    def joined(parts):
+        whole, *rest = parts
+        if rest:
+            half = rest[0].shape[0]
+            whole = jnp.concatenate([whole[:half] + rest[0], whole[half:]])
+        return whole
+
+    def scattered(parts):
+        return lax.psum_scatter(joined(parts), "wide", scatter_dimension=0, tiled=True)
+
+    hidden_shard = jnp.stack(
+        [scattered(parts) for parts in (down_grads[1], up_grads[1], down_grads[0], up_grads[0])]
+    )
+    cross_pair = tuple(first + second for first, second in zip(*cross_weight))
+    shards = dp_count * wide_count
+    attn_grad = jnp.stack(
+        [
+            jnp.concatenate(list(block), axis=1).reshape(
+                shards, -1, 128
+            )
+            for block in (source_norm_weight, tgt_weight, cross_pair)
+        ],
+        axis=1,
+    )
     norm_grad = jnp.stack(gain_parts + shift_parts)
     embed_low = (
         math.sqrt(model_width) * jnp.concatenate([source_input_gradient, tgt_in_grad], axis=0)
@@ -440,12 +553,22 @@
     embed_part = table_grad.at[jnp.clip(local_ids, 0, vocab_shard - 1)].add(
         jnp.where(inside_rows[:, None], spread_rows.astype(jnp.float32), 0.0)
     )
-    attn_shard = lax.psum_scatter(attn_grad, ("dp", "wide"), scatter_dimension=1, tiled=True)
-    up_shard, down_shard = (
-        lax.psum_scatter(up_grad, "wide", scatter_dimension=2, tiled=True),
-        lax.psum_scatter(down_grad, "wide", scatter_dimension=1, tiled=True),
-    )
-    up_sum, down_sum, embed_sum = lax.psum((up_shard, down_shard, embed_part), "dp")
+    attn_shard = (
+        lax.psum_scatter(
+            lax.psum_scatter(
+                attn_grad.reshape(-1, 128), "dp", scatter_dimension=0, tiled=True
+            ),
+            "wide",
+            scatter_dimension=0,
+            tiled=True,
+        )
+        .reshape(attn_master.shape)
+        .astype(jnp.float32)
+    )
+    hidden_sum = lax.psum(hidden_shard, "dp")
+    embed_sum = lax.psum(embed_part.astype(jnp.bfloat16), "dp").astype(jnp.float32)
+    down_sum = jnp.stack([hidden_sum[2], hidden_sum[0]])
+    up_sum = jnp.stack([hidden_sum[3].T, hidden_sum[1].T])
     square_part = (
         jnp.sum(attn_shard * attn_shard)
         + (jnp.sum(up_sum * up_sum) + jnp.sum(down_sum * down_sum) + jnp.sum(embed_sum * embed_sum))

time: 2060 us -> 1650 us (0.80)
  matrix products: 421 us -> 119 us
  waiting for transfers between devices: 1180 us -> 945 us
  Pallas kernels: 0 us -> 112 us
  local copies, waits for them, and re-layouts: 113 us -> 204 us
  blocking collectives: 95.9 us -> 55 us
  other arithmetic: 221 us -> 181 us
    unnamed x14 -> x17, waiting for transfers between devices: 265 us -> 1.46 us
    reduce_scatter x2 -> x6, waiting for transfers between devices: 245 us -> 406 us  [the longest x4 262 us: scattered(): lax.psum_scatter(joined(parts), 'wide', scatter_dimension=0, tiled=True)]
    dot_general x35 -> x19, matrix products: 187 us -> 36.6 us  [dot_rows(): lax.dot_general(left, right, (((1,), (1,)), ((), ())), preferred_element_...]
    dot_general x27 -> x19, matrix products: 141 us -> 21.6 us  [dot_cols(): lax.dot_general(left, right, (((0,), (0,)), ((), ())), preferred_element_...]
    pallas_call x0 -> x2, Pallas kernels: none -> 112 us  [the longest x1 63.2 us: head_grads(): pl.pallas_call(functools.partial(head_grads_kernel, block), out_shape=(ja...]
    psum x1 -> x2, waiting for transfers between devices: 273 us -> 209 us  [the longest x1 111 us: local(): lax.psum(embed_part.astype(jnp.bfloat16), 'dp').astype(jnp.float32)]
    unnamed x565 -> x538, local copies, waits for them, and re-layouts: 37.9 us -> 84.1 us
    all_gather x4 -> x1, blocking collectives: 55.9 us -> 14.7 us  [merged(): gathered = lax.all_gather(jnp.stack(part), axis)]
  transfers between devices with their start and end apart: 13 -> 17, of which waited for: 12 -> 15; matrix products, arithmetic and copies ran while one was open for 9% -> 14% of each run, Pallas kernels for 0% -> 0%
where the time goes in v1:
time: 1650 us; the launch traced here: 1640 us
  waiting for transfers between devices  945 us (57%)
  local copies, waits for them, and re-layouts  204 us (12%)
  other arithmetic  181 us (11%)
  matrix products  119 us (7%)
  Pallas kernels  112 us (7%)
  blocking collectives  55 us (3%)
  between operations  25.1 us (2%)
    reduce_scatter x4, waiting for transfers between devices, scattered(): lax.psum_scatter(joined(parts), 'wide', scatter_dimension=0, tiled=True)  262 us
    reduce_scatter x1, waiting for transfers between devices, local(): lax.psum_scatter(attn_grad.reshape(-1, 128), 'dp', scatter_dimension=0, t...  144 us
    psum x1, waiting for transfers between devices, local(): lax.psum(embed_part.astype(jnp.bfloat16), 'dp').astype(jnp.float32)  111 us
    psum x1, waiting for transfers between devices, local(): hidden_sum = lax.psum(hidden_shard, 'dp')  98.3 us
    unnamed x538, local copies, waits for them, and re-layouts  84.1 us
    all_gather x1, waiting for transfers between devices, local(): lax.all_gather(down_master.astype(jnp.bfloat16), 'wide', axis=1, tiled=True)  72.9 us
    reduce_scatter x1, waiting for transfers between devices, local(): lax.psum_scatter(jnp.where(inside[:, None], found_rows, 0.0).astype(jnp.b...  69.9 us
    pallas_call x1, Pallas kernels, head_grads(): pl.pallas_call(functools.partial(head_grads_kernel, block), out_shape=(ja...  63.2 us
  transfers between devices with their start and end apart: 17, of which 15 were waited for; matrix products, arithmetic and copies ran while one was open for 14% of the time, Pallas kernels for 0%

profile of v1, /device:TPU:0, one launch (start us, length us, event | category | flops | bytes accessed | tf_op | source)
XLA Modules:
  0.0 1643.4 jit_solution(169605698057400390)
XLA Ops:
  8.8 9.1 copy.288
  17.9 7.8 copy.309.table_ref
  26.4 21.1 %gather_fusion = bf16[4096,640]{1,0:T(8,128)(2,1)} fusion(bf16[4096,640]{1,0:T(8,128)(2,1)} %copy.309.table_ref, s32[4096]{0:T(1024)S(1)} %broadcast_clamp_fusion), kind=kCustom, calls=%fused_computation | custom fusion | bytes 10502144 | tf_op jit(solution)/shard_map/jit(_take)/gather | solution.py:341
  47.5 5.9 select_convert_fusion
  62.8 69.9 %reduce-scatter.10.cloned.1.call-done = bf16[512,640]{1,0:T(8,128)(2,1)} async-done(((bf16[4096,640]{1,0:T(8,128)(2,1)}), bf16[512,640]{1,0:T(8,128)(2,1)}) %reduce-scatter.10.cloned.1.call-update) | async-done | bytes 655376 | tf_op jit(solution)/shard_map/reduce_scatter | solution.py:344
  134.9 40.6 %all-gather.9.cloned.1.call-done = bf16[3,640,2048]{2,0,1:T(4,128)(2,1)} async-done(((bf16[3,20,2048]{2,0,1:T(4,128)(2,1)}), bf16[3,640,2048]{2,0,1:T(4,128)(2,1)}) %all-gather.9.cloned.1.call-update) | async-done | bytes 7864336 | tf_op jit(solution)/shard_map/all_gather | solution.py:322
  175.5 24.9 %fusion.167 = (bf16[1,640,2048]{2,0,1:T(2,128)(2,1)}, bf16[1,640,2048]{2,0,1:T(2,128)(2,1)S(1)}, bf16[1,640,2048]{2,0,1:T(2,128)(2,1)}) fusion(bf16[3,640,2048]{2,0,1:T(4,128)(2,1)} %all-gather.9.cloned.1.call-done), kind=kLoop, calls=%fused_computation.447 | loop fusion | bytes 15728640 | tf_op jit(solution)/shard_map/slice | solution.py:359
  210.0 5.8 copy.400
  233.9 19.7 %all-gather.11.cloned.1.call-done = bf16[2,640,3072]{2,1,0:T(8,128)(2,1)} async-done(((bf16[2,640,384]{2,1,0:T(8,128)(2,1)}), bf16[2,640,3072]{2,1,0:T(8,128)(2,1)}) %all-gather.11.cloned.1.call-update) | async-done | bytes 7864336 | tf_op jit(solution)/shard_map/all_gather | solution.py:324
  253.6 5.4 fusion.13
  259.0 72.9 %all-gather.13.cloned.1.call-done = bf16[2,3072,640]{2,1,0:T(8,128)(2,1)} async-done(((bf16[2,384,640]{2,1,0:T(8,128)(2,1)}), bf16[2,3072,640]{2,1,0:T(8,128)(2,1)}) %all-gather.13.cloned.1.call-update) | async-done | bytes 7864336 | tf_op jit(solution)/shard_map/all_gather | solution.py:325
  380.9 28.5 %all-gather.15.cloned.1.call-done = bf16[2048,640]{1,0:T(8,128)(2,1)} async-done(((bf16[256,640]{1,0:T(8,128)(2,1)}), bf16[2048,640]{1,0:T(8,128)(2,1)}) %all-gather.15.cloned.1.call-update) | async-done | bytes 2621456 | tf_op jit(solution)/shard_map/all_gather | solution.py:405
  412.8 31.7 %all-gather.17.cloned.1.call-done = bf16[2048,640]{1,0:T(8,128)(2,1)} async-done(((bf16[256,640]{1,0:T(8,128)(2,1)}), bf16[2048,640]{1,0:T(8,128)(2,1)}) %all-gather.17.cloned.1.call-update) | async-done | bytes 2621456 | tf_op jit(solution)/shard_map/all_gather | solution.py:406
  447.9 48.8 %head_stats.1 = (bf16[4096,4096]{1,0:T(8,128)(2,1)}, f32[8,4,4096]{2,1,0:T(4,128)}) custom-call(s32[1]{0:T(128)} %bitcast.offset_ref, bf16[4096,640]{1,0:T(8,128)(2,1)} %copy.309.table_ref, bf16[4096,640]{1,0:T(8,128)(2,1)} %constant_dynamic-update-slice_fusion.z_ref, s32[1,4096]{1,0:T(1,128)} %bitcast.419), custom_call_target="tpu_custom_call" | custom-call | tf_op jit(solution)/shard_map/head_stats/pallas_call | solution.py:182
  500.3 14.7 all-gather.1
  518.2 63.2 %head_grads.1 = (bf16[4096,640]{1,0:T(8,128)(2,1)}, f32[4096,640]{1,0:T(8,128)}) custom-call(s32[1]{0:T(128)} %bitcast.offset_ref, bf16[4096,4096]{1,0:T(8,128)(2,1)} %get-tuple-element.28.exp_ref, bf16[640,4096]{1,0:T(8,128)(2,1)} %bitcast.312, bf16[4096,640]{1,0:T(8,128)(2,1)} %constant_dynamic-update-slice_fusion.z_ref, s32[1,4096]{1,0:T(1,128)} %bitcast.420, ...), custom_call_target="tpu_custom_call" | custom-call | tf_op jit(solution)/shard_map/head_grads/pallas_call | solution.py:246
  581.4 5.3 fusion.168
  587.7 35.8 %reduce-scatter.14.cloned.1.call-done = bf16[256,640]{1,0:T(8,128)(2,1)} async-done(((bf16[2048,640]{1,0:T(8,128)(2,1)}), bf16[256,640]{1,0:T(8,128)(2,1)}) %reduce-scatter.14.cloned.1.call-update) | async-done | bytes 327696 | tf_op jit(solution)/shard_map/reduce_scatter | solution.py:448
  629.1 4.1 multiply_reduce_fusion.6
  633.3 29.5 %reduce-scatter.12.cloned.1.call-done = bf16[256,640]{1,0:T(8,128)(2,1)} async-done(((bf16[2048,640]{1,0:T(8,128)(2,1)}), bf16[256,640]{1,0:T(8,128)(2,1)}) %reduce-scatter.12.cloned.1.call-update) | async-done | bytes 327696 | tf_op jit(solution)/shard_map/reduce_scatter | solution.py:445
  662.8 4.1 fusion.76
  667.0 4.0 fusion.11
  671.0 5.0 multiply_reduce_fusion.7
  740.2 4.8 fusion.151
  751.9 3.7 pad_maximum_fusion.3
  761.2 3.6 pad_maximum_fusion.2
  772.6 3.7 pad_maximum_fusion.1
  787.5 6.9 stack_reshape.11
  799.4 6.9 stack_reshape.10
  811.3 6.7 stack_reshape.9
  818.1 11.3 pad_maximum_fusion
  830.0 38.2 %scatter_custom_fusion = f32[4096,640]{1,0:T(8,128)} fusion(f32[4096,640]{1,0:T(8,128)} %get-tuple-element.30, s32[4096]{0:T(1024)} %bitcast.426, bf16[4096,640]{1,0:T(8,128)(2,1)} %all-gather.19.cloned.1.call-done, f32[]{:T(128)} %constant.60.clone.1, pred[4096]{0:T(1024)(128)(4,1)S(1)} %bitcast.434), kind=kCustom, calls=%fused_computation.11 | custom fusion | flops 7864320 | bytes 15733248 | tf_op jit(solution)/shard_map/scatter-add | solution.py:553
  868.2 6.9 convert_element_type.417
  875.2 5.7 reduce-scatter.26.cloned.1.call-done
  880.9 85.9 %reduce-scatter.24.cloned.1.call-done = f32[384,640]{1,0:T(8,128)} async-done(((f32[3072,640]{1,0:T(8,128)}), f32[384,640]{1,0:T(8,128)}) %reduce-scatter.24.cloned.1.call-update) | async-done | bytes 983056 | tf_op jit(solution)/shard_map/reduce_scatter | solution.py:530
  966.8 85.4 %reduce-scatter.22.cloned.1.call-done = f32[384,640]{1,0:T(8,128)} async-done(((f32[3072,640]{1,0:T(8,128)}), f32[384,640]{1,0:T(8,128)}) %reduce-scatter.22.cloned.1.call-update) | async-done | bytes 983056 | tf_op jit(solution)/shard_map/reduce_scatter | solution.py:530
  1052.2 85.2 %reduce-scatter.20.cloned.1.call-done = f32[384,640]{1,0:T(8,128)} async-done(((f32[3072,640]{1,0:T(8,128)}), f32[384,640]{1,0:T(8,128)}) %reduce-scatter.20.cloned.1.call-update) | async-done | bytes 983056 | tf_op jit(solution)/shard_map/reduce_scatter | solution.py:530
  1137.4 4.3 pad_maximum_fusion.7
  1141.7 143.7 %reduce-scatter.16.cloned.1.call-done = f32[7680,128]{1,0:T(8,128)} async-done(((f32[30720,128]{1,0:T(8,128)}), f32[7680,128]{1,0:T(8,128)}) %reduce-scatter.16.cloned.1.call-update) | async-done | bytes 3932176 | tf_op jit(solution)/shard_map/reduce_scatter | solution.py:558
  1299.2 111.1 %all-reduce.7.cloned.1.call-done = bf16[4096,640]{1,0:T(8,128)(2,1)} async-done(((bf16[4096,640]{1,0:T(8,128)(2,1)}), bf16[4096,640]{1,0:T(8,128)(2,1)}) %all-reduce.7.cloned.1.call-update) | async-done | bytes 5242896 | tf_op jit(solution)/shard_map/psum | solution.py:569
  1410.3 5.8 fusion.2
  1416.1 98.3 %all-reduce.5.cloned.1.call-done = f32[4,384,640]{2,1,0:T(8,128)} async-done(((f32[4,384,640]{2,1,0:T(8,128)}), f32[4,384,640]{2,1,0:T(8,128)}) %all-reduce.5.cloned.1.call-update) | async-done | bytes 3932176 | tf_op jit(solution)/shard_map/psum | solution.py:568
  1524.3 40.4 %all-reduce.1 = (f32[2]{0:T(128)}, f32[]{:T(128)}, f32[14,640]{1,0:T(8,128)S(1)}) all-reduce(f32[2]{0:T(128)S(1)} %get-tuple-element.264, f32[]{:T(128)S(6)} %add.606, f32[14,640]{1,0:T(8,128)S(1)} %stack.101), channel_id=1, replica_groups=mesh['dp'=4,'wide'=8] {'dp','wide'}, use_global_device_ids=true, to_apply=%region_39.40 | all-reduce | flops 8963 | bytes 71704 | tf_op jit(solution)/shard_map/psum | solution.py:577
  1569.6 6.8 fusion.162
  1584.9 27.5 %fusion.157 = (bf16[4096,640]{1,0:T(8,128)(2,1)}, f32[4096,640]{1,0:T(8,128)}, f32[4096,640]{1,0:T(8,128)}, f32[4096,640]{1,0:T(8,128)}) fusion(f32[4096,640]{1,0:T(8,128)} %param.39, bf16[4096,640]{1,0:T(8,128)(2,1)} %all-reduce.7.cloned.1.call-done, f32[]{:T(128)S(6)} %div.254, f32[4096,640]{1,0:T(8,128)} %param.41, f32[4096,640]{1,0:T(8,128)} %param.40), kind=kLoop, calls=%fused_computation.443 | loop fusion | flops 41943040 | bytes 73400320 | tf_op jit(solution)/shard_map/convert_element_type | solution.py:620
  1612.4 6.0 multiply_add_fusion
  1618.4 5.1 copy.347
  1626.4 6.6 fusion.160
  (814 shorter events, 250.0 us)
Async XLA Ops:
  8.0 124.6 %reduce-scatter.10.cloned.1.call-start = ((), (), s32[]{:S(2)}) async-start(), calls=%async_computation.9 | async-start | bytes 5898240 | tf_op jit(solution)/shard_map/reduce_scatter | solution.py:344
  26.4 21.1 %copy-start.159 = (pred[1,4,8,128]{3,1,2,0:T(4,128)(4,1)}, pred[1,4,8,128]{3,1,2,0:T(4,128)(4,1)S(1)}, u32[]{:S(2)}) copy-start(pred[1,4,8,128]{3,1,2,0:T(4,128)(4,1)S(1)} %copy.379) | copy-start | bytes 12292
  53.5 122.0 %all-gather.9.cloned.1.call-start = ((), (), s32[]{:S(2)}) async-start(), calls=%async_computation.10 | async-start | bytes 10813440 | tf_op jit(solution)/shard_map/all_gather | solution.py:322
  55.5 198.1 %all-gather.11.cloned.1.call-start = ((), (), s32[]{:S(2)}) async-start(), calls=%async_computation.11 | async-start | bytes 8847360 | tf_op jit(solution)/shard_map/all_gather | solution.py:324
  56.7 275.2 %all-gather.13.cloned.1.call-start = ((), (), s32[]{:S(2)}) async-start(), calls=%async_computation.12 | async-start | bytes 8847360 | tf_op jit(solution)/shard_map/all_gather | solution.py:325
  59.3 74.5 %copy-start.13 = (f32[256,640]{1,0:T(8,128)S(1)}, f32[256,640]{1,0:T(8,128)}, u32[]{:S(2)}) copy-start(f32[256,640]{1,0:T(8,128)} %constant.152.clone) | copy-start | bytes 1966084
  59.4 350.0 %all-gather.15.cloned.1.call-start = ((), (), s32[]{:S(2)}) async-start(), calls=%async_computation.13 | async-start | bytes 2949120 | tf_op jit(solution)/shard_map/all_gather | solution.py:405
  59.5 74.6 %copy-start.206 = (pred[256]{0:T(512)(128)(4,1)}, pred[256]{0:T(512)(128)(4,1)S(1)}, u32[]{:S(2)}) copy-start(pred[256]{0:T(512)(128)(4,1)S(1)} %compare_reduce_fusion) | copy-start | bytes 772
  62.6 71.9 %copy-start.155 = (f32[640]{0:T(1024)}, f32[640]{0:T(1024)S(1)}, u32[]{:S(2)}) copy-start(f32[640]{0:T(1024)S(1)} %get-tuple-element.208) | copy-start | bytes 7684
  62.7 71.9 %copy-start.157 = (f32[640]{0:T(1024)}, f32[640]{0:T(1024)S(1)}, u32[]{:S(2)}) copy-start(f32[640]{0:T(1024)S(1)} %get-tuple-element.210) | copy-start | bytes 7684
  134.5 65.9 %copy-start.209 = (f32[256]{0:T(256)}, f32[256]{0:T(256)S(1)}, u32[]{:S(2)}) copy-start(f32[256]{0:T(256)S(1)} %add_rsqrt_fusion.8) | copy-start | bytes 3076
  134.5 65.9 %copy-start.211 = (f32[256]{0:T(256)}, f32[256]{0:T(256)S(1)}, u32[]{:S(2)}) copy-start(f32[256]{0:T(256)S(1)} %add_rsqrt_fusion.9) | copy-start | bytes 3076
  134.9 70.1 %copy-start.78 = (bf16[256,640]{1,0:T(8,128)(2,1)}, bf16[256,640]{1,0:T(8,128)(2,1)S(1)}, u32[]{:S(2)}) copy-start(bf16[256,640]{1,0:T(8,128)(2,1)S(1)} %get-tuple-element.248) | copy-start | bytes 983044
  134.9 85.5 %copy-start.76 = (bf16[256,640]{1,0:T(8,128)(2,1)}, bf16[256,640]{1,0:T(8,128)(2,1)S(1)}, u32[]{:S(2)}) copy-start(bf16[256,640]{1,0:T(8,128)(2,1)S(1)} %get-tuple-element.247) | copy-start | bytes 983044
  205.0 10.8 slice-start
  229.8 23.8 %copy-start.202 = (f32[256]{0:T(256)}, f32[256]{0:T(256)S(1)}, u32[]{:S(2)}) copy-start(f32[256]{0:T(256)S(1)} %add_rsqrt_fusion.7) | copy-start | bytes 3076
  230.8 22.8 %copy-start.180 = (f32[256]{0:T(256)S(1)}, f32[256]{0:T(256)}, u32[]{:S(2)}) copy-start(f32[256]{0:T(256)} %copy-done.179) | copy-start | bytes 3076
  253.6 78.3 %copy-start.171 = (pred[1536]{0:T(1024)(128)(4,1)S(1)}, pred[1536]{0:T(1024)(128)(4,1)}, u32[]{:S(2)}) copy-start(pred[1536]{0:T(1024)(128)(4,1)} %iota_compare_fusion.2) | copy-start | bytes 4612
  259.0 76.5 %copy-start.153 = (f32[640]{0:T(1024)S(1)}, f32[640]{0:T(1024)}, u32[]{:S(2)}) copy-start(f32[640]{0:T(1024)} %get-tuple-element.203) | copy-start | bytes 7684
  338.9 9.1 copy-start.208
  338.9 10.9 copy-start.173
  340.2 9.6 copy-start.190
  356.9 305.9 %copy-start.151 = (f32[256]{0:T(256)}, f32[256]{0:T(256)S(1)}, u32[]{:S(2)}) copy-start(f32[256]{0:T(256)S(1)} %broadcast_multiply_fusion.21) | copy-start | bytes 3076
  358.6 16.5 %copy-start.175 = (f32[256]{0:T(256)}, f32[256]{0:T(256)S(1)}, u32[]{:S(2)}) copy-start(f32[256]{0:T(256)S(1)} %add_rsqrt_fusion) | copy-start | bytes 3076
  374.9 301.1 %copy-start.161 = (f32[256]{0:T(256)}, f32[256]{0:T(256)S(1)}, u32[]{:S(2)}) copy-start(f32[256]{0:T(256)S(1)} %broadcast_multiply_fusion.24) | copy-start | bytes 3076
  376.8 67.7 %all-gather.17.cloned.1.call-start = ((), (), s32[]{:S(2)}) async-start(), calls=%async_computation.14 | async-start | bytes 2949120 | tf_op jit(solution)/shard_map/all_gather | solution.py:406
  377.5 246.0 %reduce-scatter.14.cloned.1.call-start = ((), (), s32[]{:S(2)}) async-start(), calls=%async_computation.16 | async-start | bytes 2949120 | tf_op jit(solution)/shard_map/reduce_scatter | solution.py:448
  380.2 32.6 %copy-start.149 = (f32[2048]{0:T(1024)}, f32[2048]{0:T(1024)S(1)}, u32[]{:S(2)}) copy-start(f32[2048]{0:T(1024)S(1)} %broadcast_divide_fusion) | copy-start | bytes 24580
  586.7 36.8 %copy-start.176 = (f32[256]{0:T(256)S(1)}, f32[256]{0:T(256)}, u32[]{:S(2)}) copy-start(f32[256]{0:T(256)} %copy-done.175) | copy-start | bytes 3076
  586.8 38.9 %copy-start.172 = (pred[1536]{0:T(1024)(128)(4,1)S(1)}, pred[1536]{0:T(1024)(128)(4,1)}, u32[]{:S(2)}) copy-start(pred[1536]{0:T(1024)(128)(4,1)} %iota_compare_fusion.2) | copy-start | bytes 4612
  586.8 76.0 %reduce-scatter.12.cloned.1.call-start = ((), (), s32[]{:S(2)}) async-start(), calls=%async_computation.15 | async-start | bytes 2949120 | tf_op jit(solution)/shard_map/reduce_scatter | solution.py:445
  587.4 242.3 %all-gather.19.cloned.1.call-start = ((), (), s32[]{:S(2)}) async-start(), calls=%async_computation.24 | async-start | bytes 5898240 | tf_op jit(solution)/shard_map/all_gather | solution.py:550
  625.7 37.1 %copy-start.219 = (f32[256]{0:T(256)}, f32[256]{0:T(256)S(1)}, u32[]{:S(2)}) copy-start(f32[256]{0:T(256)S(1)} %broadcast_multiply_fusion.13) | copy-start | bytes 3076
  625.7 37.1 %copy-start.221 = (f32[256]{0:T(256)}, f32[256]{0:T(256)S(1)}, u32[]{:S(2)}) copy-start(f32[256]{0:T(256)S(1)} %broadcast_multiply_fusion.14) | copy-start | bytes 3076
  629.1 33.7 %copy-start.185 = (f32[256]{0:T(256)S(1)}, f32[256]{0:T(256)}, u32[]{:S(2)}) copy-start(f32[256]{0:T(256)} %copy-done.184) | copy-start | bytes 3076
  666.9 9.1 copy-start.223
  667.0 9.1 copy-start.225
  709.5 10.0 slice-start.10
  739.4 141.6 %reduce-scatter.26.cloned.1.call-start = ((), (), s32[]{:S(2)}) async-start(), calls=%async_computation.22 | async-start | bytes 8847360 | tf_op jit(solution)/shard_map/reduce_scatter | solution.py:530
  745.0 221.8 %reduce-scatter.24.cloned.1.call-start = ((), (), s32[]{:S(2)}) async-start(), calls=%async_computation.21 | async-start | bytes 8847360 | tf_op jit(solution)/shard_map/reduce_scatter | solution.py:530
  755.7 296.5 %reduce-scatter.22.cloned.1.call-start = ((), (), s32[]{:S(2)}) async-start(), calls=%async_computation.20 | async-start | bytes 8847360 | tf_op jit(solution)/shard_map/reduce_scatter | solution.py:530
  764.8 372.5 %reduce-scatter.20.cloned.1.call-start = ((), (), s32[]{:S(2)}) async-start(), calls=%async_computation.19 | async-start | bytes 8847360 | tf_op jit(solution)/shard_map/reduce_scatter | solution.py:530
  776.3 509.1 %reduce-scatter.16.cloned.1.call-start = ((), (), s32[]{:S(2)}) async-start(), calls=%async_computation.17 | async-start | bytes 19660800 | tf_op jit(solution)/shard_map/reduce_scatter | solution.py:558
  829.4 581.0 %all-reduce.7.cloned.1.call-start = ((), (), s32[]{:S(2)}) async-start(), calls=%async_computation.25 | async-start | bytes 10485760 | tf_op jit(solution)/shard_map/psum | solution.py:569
  875.1 639.3 %all-reduce.5.cloned.1.call-start = ((), (), s32[]{:S(2)}) async-start(), calls=%async_computation.23 | async-start | bytes 7864320 | tf_op jit(solution)/shard_map/psum | solution.py:568
  1141.7 145.3 %copy-start.58 = (f32[2,640,384]{2,1,0:T(8,128)S(1)}, f32[2,640,384]{2,1,0:T(8,128)}, u32[]{:S(2)}) copy-start(f32[2,640,384]{2,1,0:T(8,128)} %param.33) | copy-start | bytes 5898244
  1141.7 380.2 %reduce-scatter.18.cloned.1.call-start = ((), (), s32[]{:S(2)}) async-start(), calls=%async_computation.18 | async-start | bytes 4423680 | tf_op jit(solution)/shard_map/reduce_scatter | solution.py:557
  1584.9 27.5 %copy-start.19 = (f32[4096,160]{1,0:T(8,128)S(1)}, f32[4096,160]{1,0:T(8,128)}, u32[]{:S(2)}) copy-start(f32[4096,160]{1,0:T(8,128)} %copy.343) | copy-start | bytes 7864324
  (226 other events, 580.1 us)
Sparse Core Ops, SparseCore 0:
  53.6 78.9 reduce-scatter.9
  376.9 32.4 all-gather.14
  411.6 32.8 all-gather.16
  586.9 36.6 reduce-scatter.13
  626.2 36.4 reduce-scatter.11
  739.5 55.0 all-gather.18
  797.5 83.4 reduce-scatter.25
  883.8 82.9 reduce-scatter.23
  969.1 82.9 reduce-scatter.21
  1054.3 82.9 reduce-scatter.19
  1140.5 144.8 reduce-scatter.15
  1289.1 121.1 all-reduce.6
  1414.0 100.3 all-reduce.4
Sparse Core Ops, SparseCore 1:
  57.4 118.0 all-gather.8
  177.5 76.0 all-gather.10
  255.7 76.1 all-gather.12
  1285.5 47.3 reduce-scatter.17

commit v2 on v1

--- a/solution.py
+++ b/solution.py
@@ -15,6 +15,7 @@
 V = 32768
 
 
+MESH = pl.DeviceIdType.MESH
 smooth = 0.1
 norm_eps = 1e-05
 clip_limit = 0.005
@@ -274,6 +275,169 @@
     )
 
 
+def reduce_kernel(*refs):
+    hidden, attn, (hidden_out, attn_out) = refs[:4], refs[4], refs[5:7]
+    own_f, own_a, sib_f, sib_a, plane_f, plane_a, far_f, far_a = refs[7:15]
+    load_sem, pair_send, pair_recv, plane_send, plane_recv, far_send, far_recv = refs[15:]
+    f32 = jnp.float32
+    dp, wide = lax.axis_index("dp"), lax.axis_index("wide")
+    level, core = wide // 2, wide % 2
+    sibling = (dp, level * 2 + 1 - core)
+    row, col = dp // 2, dp % 2
+    peers = (row * 2 + 1 - col, (1 - row) * 2 + col, (1 - row) * 2 + 1 - col)
+    far = [lax.rem(level + 1 + j, 4) for j in range(4)]
+
+    barrier = pltpu.get_barrier_semaphore()
+    partners = [sibling] + [(p, wide) for p in peers] + [(dp, far[j] * 2 + core) for j in range(3)]
+    for device in partners:
+        pl.semaphore_signal(barrier, inc=1, device_id=device, device_id_type=MESH)
+    pl.semaphore_wait(barrier, len(partners))
+
+    def remote(src, dst, send, recv, device):
+        copy = pltpu.make_async_remote_copy(
+            src_ref=src, dst_ref=dst, send_sem=send, recv_sem=recv, device_id=device, device_id_type=MESH
+        )
+        copy.start()
+        return copy
+
+    pair, loads = [], []
+    for j in range(4):
+        mine, theirs = far[j] * 2 + core, far[j] * 2 + 1 - core
+        for k in range(4):
+            pair.append(
+                remote(hidden[k].at[theirs], sib_f.at[j, k], pair_send.at[j, k], pair_recv.at[j, k], sibling)
+            )
+            load = pltpu.make_async_copy(hidden[k].at[mine], own_f.at[j, k], load_sem.at[j, k])
+            load.start()
+            loads.append(load)
+        pair.append(
+            remote(attn.at[:, theirs], sib_a.at[j], pair_send.at[j, 4], pair_recv.at[j, 4], sibling)
+        )
+        load = pltpu.make_async_copy(attn.at[:, mine], own_a.at[j], load_sem.at[j, 4])
+        load.start()
+        loads.append(load)
+
+    plane = []
+    for j in range(4):
+        for index in range(5):
+            loads[5 * j + index].wait()
+            pair[5 * j + index].wait_recv()
+
+        def add_f(k, carry):
+            for q in range(4):
+                own_f[j, k, q] = (own_f[j, k, q].astype(f32) + sib_f[j, k, q].astype(f32)).astype(jnp.bfloat16)
+            return carry
+
+        lax.fori_loop(0, 4, add_f, 0)
+
+        def add_a(q, carry):
+            own_a[j, q] = (own_a[j, q].astype(f32) + sib_a[j, q].astype(f32)).astype(jnp.bfloat16)
+            return carry
+
+        lax.fori_loop(0, 4, add_a, 0)
+        sent = []
+        for p, peer in enumerate(peers):
+            sent.append(
+                (
+                    remote(own_f.at[j, :, peer], plane_f.at[j, p], plane_send.at[j, p, 0], plane_recv.at[j, p, 0], (peer, wide)),
+                    remote(own_a.at[j, peer], plane_a.at[j, p], plane_send.at[j, p, 1], plane_recv.at[j, p, 1], (peer, wide)),
+                )
+            )
+        plane.append(sent)
+
+    flown = []
+    for j in range(4):
+        for sent in plane[j]:
+            for copy in sent:
+                copy.wait_recv()
+
+        def total_f(k):
+            total = own_f[j, k, dp].astype(f32)
+            for p in range(3):
+                total += plane_f[j, p, k].astype(f32)
+            return total
+
+        def total_a():
+            total = own_a[j, dp].astype(f32)
+            for p in range(3):
+                total += plane_a[j, p].astype(f32)
+            return total
+
+        if j < 3:
+
+            def keep(k, carry):
+                plane_f[j, 0, k] = total_f(k).astype(jnp.bfloat16)
+                return carry
+
+            lax.fori_loop(0, 4, keep, 0)
+            plane_a[j, 0] = total_a().astype(jnp.bfloat16)
+            device = (dp, far[j] * 2 + core)
+            flown.append(
+                (
+                    remote(plane_f.at[j, 0], far_f.at[j], far_send.at[j, 0], far_recv.at[j, 0], device),
+                    remote(plane_a.at[j, 0], far_a.at[j], far_send.at[j, 1], far_recv.at[j, 1], device),
+                )
+            )
+        else:
+
+            def last(k, carry):
+                hidden_out[k] = total_f(k)
+                return carry
+
+            lax.fori_loop(0, 4, last, 0)
+            attn_out[...] = total_a()
+    for j in range(3):
+        for copy in flown[j]:
+            copy.wait_recv()
+
+        def finish(k, carry):
+            hidden_out[k] += far_f[j, k].astype(f32)
+            return carry
+
+        lax.fori_loop(0, 4, finish, 0)
+        attn_out[...] += far_a[j].astype(f32)
+    for copy in pair:
+        copy.wait_send()
+    for sent in plane:
+        for both in sent:
+            for copy in both:
+                copy.wait_send()
+    for both in flown:
+        for copy in both:
+            copy.wait_send()
+
+
+def reduced(hidden, attn, cid):
+    _, _, rows, width = hidden[0].shape
+    lines = attn.shape[2]
+    bf = jnp.bfloat16
+    hbm = pl.BlockSpec(memory_space=pltpu.HBM)
+    vmem = pl.BlockSpec(memory_space=pltpu.VMEM)
+    dma = pltpu.SemaphoreType.DMA
+    return pl.pallas_call(
+        reduce_kernel,
+        out_shape=(
+            jax.ShapeDtypeStruct((4, rows, width), jnp.float32),
+            jax.ShapeDtypeStruct((lines, 128), jnp.float32),
+        ),
+        in_specs=[hbm] * 5,
+        out_specs=(vmem, vmem),
+        scratch_shapes=[
+            pltpu.VMEM((4, 4, 4, rows, width), bf),
+            pltpu.VMEM((4, 4, lines, 128), bf),
+            pltpu.VMEM((4, 4, 4, rows, width), bf),
+            pltpu.VMEM((4, 4, lines, 128), bf),
+            pltpu.VMEM((4, 3, 4, rows, width), bf),
+            pltpu.VMEM((4, 3, lines, 128), bf),
+            pltpu.VMEM((3, 4, rows, width), bf),
+            pltpu.VMEM((3, lines, 128), bf),
+            dma((4, 5)), dma((4, 5)), dma((4, 5)), dma((4, 3, 2)), dma((4, 3, 2)), dma((3, 2)), dma((3, 2)),
+        ],
+        compiler_params=pltpu.CompilerParams(collective_id=cid, has_side_effects=True, vmem_limit_bytes=56 << 20),
+        name="reduce_grads",
+    )(*hidden, attn)
+
+
 def adamw(weight, first_m, second_m, grad_item, step_rate):
     first_new = beta_first * first_m + (1.0 - beta_first) * grad_item
     second_new = beta_second * second_m + (1.0 - beta_second) * grad_item * grad_item
@@ -319,6 +483,8 @@
     seq_dev = token_ids.shape[0] // (wide_count * dp_count)
     tokens = seq_dev * length
     vocab_shard = embed_master.shape[0]
+    planes = (dp_count, wide_count) == (4, 8)
+    link_type = jnp.bfloat16 if planes else jnp.float32
     attn_full = lax.all_gather(attn_master.astype(jnp.bfloat16), ("dp", "wide"), axis=1, tiled=True)
     up_full, down_full = (
         lax.all_gather(up_master.astype(jnp.bfloat16), "wide", axis=2, tiled=True),
@@ -526,19 +692,12 @@
             whole = jnp.concatenate([whole[:half] + rest[0], whole[half:]])
         return whole
 
-    def scattered(parts):
-        return lax.psum_scatter(joined(parts), "wide", scatter_dimension=0, tiled=True)
-
-    hidden_shard = jnp.stack(
-        [scattered(parts) for parts in (down_grads[1], up_grads[1], down_grads[0], up_grads[0])]
-    )
+    hidden_grads = [joined(p) for p in (down_grads[1], up_grads[1], down_grads[0], up_grads[0])]
     cross_pair = tuple(first + second for first, second in zip(*cross_weight))
     shards = dp_count * wide_count
     attn_grad = jnp.stack(
         [
-            jnp.concatenate(list(block), axis=1).reshape(
-                shards, -1, 128
-            )
+            jnp.concatenate(block, axis=1).astype(link_type).reshape(shards, -1, 128)
             for block in (source_norm_weight, tgt_weight, cross_pair)
         ],
         axis=1,
@@ -553,8 +712,31 @@
     embed_part = table_grad.at[jnp.clip(local_ids, 0, vocab_shard - 1)].add(
         jnp.where(inside_rows[:, None], spread_rows.astype(jnp.float32), 0.0)
     )
-    attn_shard = (
-        lax.psum_scatter(
+    if planes:
+        hidden_part, attn_shard = reduced(
+            [
+                part.astype(link_type).reshape(wide_count, dp_count, -1, model_width)
+                for part in hidden_grads
+            ],
+            attn_grad.reshape(dp_count, wide_count, -1, 128),
+            1,
+        )
+        hidden_sum = jnp.moveaxis(
+            lax.all_gather(hidden_part.astype(link_type), "dp"), 0, 1
+        ).reshape(4, -1, model_width).astype(jnp.float32)
+        square_part = jnp.sum(hidden_part * hidden_part)
+    else:
+        hidden_sum = lax.psum(
+            jnp.stack(
+                [
+                    lax.psum_scatter(part, "wide", scatter_dimension=0, tiled=True)
+                    for part in hidden_grads
+                ]
+            ),
+            "dp",
+        )
+        square_part = jnp.sum(hidden_sum * hidden_sum) / dp_count
+        attn_shard = lax.psum_scatter(
             lax.psum_scatter(
                 attn_grad.reshape(-1, 128), "dp", scatter_dimension=0, tiled=True
             ),
@@ -562,17 +744,12 @@
             scatter_dimension=0,
             tiled=True,
         )
-        .reshape(attn_master.shape)
-        .astype(jnp.float32)
-    )
-    hidden_sum = lax.psum(hidden_shard, "dp")
+    attn_shard = attn_shard.reshape(attn_master.shape)
     embed_sum = lax.psum(embed_part.astype(jnp.bfloat16), "dp").astype(jnp.float32)
     down_sum = jnp.stack([hidden_sum[2], hidden_sum[0]])
     up_sum = jnp.stack([hidden_sum[3].T, hidden_sum[1].T])
-    square_part = (
-        jnp.sum(attn_shard * attn_shard)
-        + (jnp.sum(up_sum * up_sum) + jnp.sum(down_sum * down_sum) + jnp.sum(embed_sum * embed_sum))
-        / dp_count
+    square_part += (
+        jnp.sum(attn_shard * attn_shard) + jnp.sum(embed_sum * embed_sum) / dp_count
     )
     square_all, norm_sum, losses = lax.psum((square_part, norm_grad, loss_own), ("dp", "wide"))
     grad_norm = jnp.sqrt(square_all + jnp.sum(norm_sum * norm_sum))

time: 1650 us -> 1270 us (0.77)
  waiting for transfers between devices: 945 us -> 431 us
  Pallas kernels: 112 us -> 252 us
  other arithmetic: 181 us -> 161 us
    reduce_scatter x6 -> x0, waiting for transfers between devices: 406 us -> none  [the longest x4 262 us: scattered(): lax.psum_scatter(joined(parts), 'wide', scatter_dimension=0, tiled=True)]
    pallas_call x0 -> x1, Pallas kernels: none -> 140 us  [reduced(): pl.pallas_call(reduce_kernel, out_shape=(jax.ShapeDtypeStruct((4, rows, w...]
    psum x1 -> x0, waiting for transfers between devices: 98.3 us -> none  [local(): hidden_sum = lax.psum(hidden_shard, 'dp')]
    unnamed x538 -> x549, local copies, waits for them, and re-layouts: 84.1 us -> 88.2 us
  transfers between devices with their start and end apart: 17 -> 11, of which waited for: 15 -> 9; matrix products, arithmetic and copies ran while one was open for 14% -> 18% of each run, Pallas kernels for 0% -> 11%
where the time goes in v2:
time: 1270 us
  waiting for transfers between devices  431 us (34%)
  Pallas kernels  252 us (20%)
  local copies, waits for them, and re-layouts  211 us (17%)
  other arithmetic  161 us (13%)
  matrix products  130 us (10%)
  blocking collectives  55.1 us (4%)
  between operations  24.7 us (2%)
    pallas_call x1, Pallas kernels, reduced(): pl.pallas_call(reduce_kernel, out_shape=(jax.ShapeDtypeStruct((4, rows, w...  140 us
    psum x1, waiting for transfers between devices, local(): lax.psum(embed_part.astype(jnp.bfloat16), 'dp').astype(jnp.float32)  101 us
    unnamed x549, local copies, waits for them, and re-layouts  88.2 us
    all_gather x1, waiting for transfers between devices, local(): lax.all_gather(down_master.astype(jnp.bfloat16), 'wide', axis=1, tiled=True)  72.8 us
    reduce_scatter x1, waiting for transfers between devices, local(): lax.psum_scatter(jnp.where(inside[:, None], found_rows, 0.0).astype(jnp.b...  70.3 us
    pallas_call x1, Pallas kernels, head_grads(): pl.pallas_call(functools.partial(head_grads_kernel, block), out_shape=(ja...  63.2 us
    pallas_call x1, Pallas kernels, head_stats(): pl.pallas_call(functools.partial(head_stats_kernel, block), out_shape=(ja...  48.9 us
    all_gather x1, waiting for transfers between devices, local(): lax.all_gather(attn_master.astype(jnp.bfloat16), ('dp', 'wide'), axis=1,...  40.6 us
  transfers between devices with their start and end apart: 11, of which 9 were waited for; matrix products, arithmetic and copies ran while one was open for 18% of the time, Pallas kernels for 11%

profile of v2, /device:TPU:0, one launch (start us, length us, event | category | flops | bytes accessed | tf_op | source)
XLA Modules:
  0.0 1265.1 jit_solution(9238022653761930136)
XLA Ops:
  9.5 9.1 copy.286
  18.6 7.8 copy.307.table_ref
  27.1 21.1 %gather_fusion = bf16[4096,640]{1,0:T(8,128)(2,1)} fusion(bf16[4096,640]{1,0:T(8,128)(2,1)} %copy.307.table_ref, s32[4096]{0:T(1024)S(1)} %broadcast_clamp_fusion), kind=kCustom, calls=%fused_computation | custom fusion | bytes 10502144 | tf_op jit(solution)/shard_map/jit(_take)/gather | solution.py:507
  48.2 5.9 select_convert_fusion
  63.1 70.3 %reduce-scatter.4.cloned.1.call-done = bf16[512,640]{1,0:T(8,128)(2,1)} async-done(((bf16[4096,640]{1,0:T(8,128)(2,1)}), bf16[512,640]{1,0:T(8,128)(2,1)}) %reduce-scatter.4.cloned.1.call-update) | async-done | bytes 655376 | tf_op jit(solution)/shard_map/reduce_scatter | solution.py:510
  135.6 40.6 %all-gather.11.cloned.1.call-done = bf16[3,640,2048]{2,0,1:T(4,128)(2,1)} async-done(((bf16[3,20,2048]{2,0,1:T(4,128)(2,1)}), bf16[3,640,2048]{2,0,1:T(4,128)(2,1)}) %all-gather.11.cloned.1.call-update) | async-done | bytes 7864336 | tf_op jit(solution)/shard_map/all_gather | solution.py:488
  176.2 24.8 %fusion.167 = (bf16[1,640,2048]{2,0,1:T(2,128)(2,1)}, bf16[1,640,2048]{2,0,1:T(2,128)(2,1)S(1)}, bf16[1,640,2048]{2,0,1:T(2,128)(2,1)}) fusion(bf16[3,640,2048]{2,0,1:T(4,128)(2,1)} %all-gather.11.cloned.1.call-done), kind=kLoop, calls=%fused_computation.454 | loop fusion | bytes 15728640 | tf_op jit(solution)/shard_map/slice | solution.py:525
  210.5 5.8 copy.396
  234.5 19.8 %all-gather.13.cloned.1.call-done = bf16[2,640,3072]{2,1,0:T(8,128)(2,1)} async-done(((bf16[2,640,384]{2,1,0:T(8,128)(2,1)}), bf16[2,640,3072]{2,1,0:T(8,128)(2,1)}) %all-gather.13.cloned.1.call-update) | async-done | bytes 7864336 | tf_op jit(solution)/shard_map/all_gather | solution.py:490
  254.3 5.4 fusion.16
  259.8 72.8 %all-gather.15.cloned.1.call-done = bf16[2,3072,640]{2,1,0:T(8,128)(2,1)} async-done(((bf16[2,384,640]{2,1,0:T(8,128)(2,1)}), bf16[2,3072,640]{2,1,0:T(8,128)(2,1)}) %all-gather.15.cloned.1.call-update) | async-done | bytes 7864336 | tf_op jit(solution)/shard_map/all_gather | solution.py:491
  332.6 3.4 fusion.180
  381.5 28.5 %all-gather.17.cloned.1.call-done = bf16[2048,640]{1,0:T(8,128)(2,1)} async-done(((bf16[256,640]{1,0:T(8,128)(2,1)}), bf16[2048,640]{1,0:T(8,128)(2,1)}) %all-gather.17.cloned.1.call-update) | async-done | bytes 2621456 | tf_op jit(solution)/shard_map/all_gather | solution.py:571
  409.9 3.5 constant_dynamic-update-slice_fusion.1
  413.4 31.7 %all-gather.19.cloned.1.call-done = bf16[2048,640]{1,0:T(8,128)(2,1)} async-done(((bf16[256,640]{1,0:T(8,128)(2,1)}), bf16[2048,640]{1,0:T(8,128)(2,1)}) %all-gather.19.cloned.1.call-update) | async-done | bytes 2621456 | tf_op jit(solution)/shard_map/all_gather | solution.py:572
  445.1 3.5 constant_dynamic-update-slice_fusion.z_ref
  448.5 48.9 %head_stats.1 = (bf16[4096,4096]{1,0:T(8,128)(2,1)}, f32[8,4,4096]{2,1,0:T(4,128)}) custom-call(s32[1]{0:T(128)} %bitcast.offset_ref, bf16[4096,640]{1,0:T(8,128)(2,1)} %copy.307.table_ref, bf16[4096,640]{1,0:T(8,128)(2,1)} %constant_dynamic-update-slice_fusion.z_ref, s32[1,4096]{1,0:T(1,128)} %bitcast.430), custom_call_target="tpu_custom_call" | custom-call | tf_op jit(solution)/shard_map/head_stats/pallas_call | solution.py:183
  500.9 14.7 %all-gather.2 = f32[8,4,4096]{2,1,0:T(4,128)S(1)} all-gather(f32[1,4,4096]{2,1,0:T(4,128)S(1)} %maximum_bitcast_fusion), channel_id=2, replica_groups=mesh['dp'=4,'wide'=8] {'wide'}, dimensions={0}, use_global_device_ids=true | all-gather | bytes 589824 | tf_op jit(solution)/shard_map/all_gather | solution.py:33
  518.8 63.2 %head_grads.1 = (bf16[4096,640]{1,0:T(8,128)(2,1)}, f32[4096,640]{1,0:T(8,128)}) custom-call(s32[1]{0:T(128)} %bitcast.offset_ref, bf16[4096,4096]{1,0:T(8,128)(2,1)} %get-tuple-element.30.exp_ref, bf16[640,4096]{1,0:T(8,128)(2,1)} %bitcast.315, bf16[4096,640]{1,0:T(8,128)(2,1)} %constant_dynamic-update-slice_fusion.z_ref, s32[1,4096]{1,0:T(1,128)} %bitcast.431, ...), custom_call_target="tpu_custom_call" | custom-call | tf_op jit(solution)/shard_map/head_grads/pallas_call | solution.py:247
  582.0 5.3 fusion.168
  588.3 35.8 %reduce-scatter.8.cloned.1.call-done = bf16[256,640]{1,0:T(8,128)(2,1)} async-done(((bf16[2048,640]{1,0:T(8,128)(2,1)}), bf16[256,640]{1,0:T(8,128)(2,1)}) %reduce-scatter.8.cloned.1.call-update) | async-done | bytes 327696 | tf_op jit(solution)/shard_map/reduce_scatter | solution.py:614
  626.4 3.3 fusion.21
  629.8 4.1 multiply_reduce_fusion.5
  633.9 29.5 %reduce-scatter.6.cloned.1.call-done = bf16[256,640]{1,0:T(8,128)(2,1)} async-done(((bf16[2048,640]{1,0:T(8,128)(2,1)}), bf16[256,640]{1,0:T(8,128)(2,1)}) %reduce-scatter.6.cloned.1.call-update) | async-done | bytes 327696 | tf_op jit(solution)/shard_map/reduce_scatter | solution.py:611
  663.4 3.2 fusion.81
  677.3 3.9 fusion.14
  681.2 5.0 multiply_reduce_fusion.6
  747.5 3.2 copy-done.14
  770.1 5.4 convert_element_type.482
  784.8 5.3 convert_element_type.481
  799.5 5.3 convert_element_type.464
  804.8 5.1 convolution_convert_fusion
  809.9 3.2 fusion.11
  813.3 3.2 fusion.10
  827.9 3.6 pad_maximum_fusion
  831.5 139.8 %reduce_grads.1 = (f32[4,96,640]{2,1,0:T(8,128)}, f32[960,128]{1,0:T(8,128)}) custom-call(bf16[8,4,96,640]{3,2,1,0:T(8,128)(2,1)} %bitcast.333, bf16[8,4,96,640]{3,2,1,0:T(8,128)(2,1)} %bitcast.334, bf16[8,4,96,640]{3,2,1,0:T(8,128)(2,1)} %bitcast.335, bf16[8,4,96,640]{3,2,1,0:T(8,128)(2,1)} %bitcast.319, bf16[4,8,960,128]{3,2,1,0:T(8,128)(2,1)} %bitcast.318), custom_call_target="tpu_custom_call" | custom-call | tf_op jit(solution)/shard_map/reduce_grads/pallas_call | solution.py:417
  974.5 37.8 %scatter_custom_fusion = f32[4096,640]{1,0:T(8,128)} fusion(f32[4096,640]{1,0:T(8,128)} %get-tuple-element.34, s32[4096]{0:T(1024)} %bitcast.437, bf16[4096,640]{1,0:T(8,128)(2,1)} %all-gather.21.cloned.1.call-done, f32[]{:T(128)} %constant.60.clone.1, pred[4096]{0:T(1024)(128)(4,1)S(1)} %bitcast.445), kind=kCustom, calls=%fused_computation.10 | custom fusion | flops 7864320 | bytes 15733248 | tf_op jit(solution)/shard_map/scatter-add | solution.py:712
  1012.3 6.9 convert_element_type.485
  1022.5 3.3 copy.338
  1029.1 3.4 copy.341
  1038.5 100.7 %all-reduce.4.cloned.1.call-done = bf16[4096,640]{1,0:T(8,128)(2,1)} async-done(((bf16[4096,640]{1,0:T(8,128)(2,1)}), bf16[4096,640]{1,0:T(8,128)(2,1)}) %all-reduce.4.cloned.1.call-update) | async-done | bytes 5242896 | tf_op jit(solution)/shard_map/psum | solution.py:748
  1139.2 5.8 fusion.2
  1147.1 40.4 %all-reduce.1 = (f32[2]{0:T(128)}, f32[]{:T(128)}, f32[14,640]{1,0:T(8,128)S(1)}) all-reduce(f32[2]{0:T(128)S(1)} %copy-done.246, f32[]{:T(128)S(6)} %add.588, f32[14,640]{1,0:T(8,128)S(1)} %stack.77), channel_id=1, replica_groups=mesh['dp'=4,'wide'=8] {'dp','wide'}, use_global_device_ids=true, to_apply=%region_39.40 | all-reduce | flops 8963 | bytes 71704 | tf_op jit(solution)/shard_map/psum | solution.py:754
  1192.2 6.5 fusion.162
  1206.2 27.5 %fusion.157 = (bf16[4096,640]{1,0:T(8,128)(2,1)}, f32[4096,640]{1,0:T(8,128)}, f32[4096,640]{1,0:T(8,128)}, f32[4096,640]{1,0:T(8,128)}) fusion(f32[4096,640]{1,0:T(8,128)} %param.39, bf16[4096,640]{1,0:T(8,128)(2,1)} %all-reduce.4.cloned.1.call-done, f32[]{:T(128)S(6)} %div.254, f32[4096,640]{1,0:T(8,128)} %param.41, f32[4096,640]{1,0:T(8,128)} %param.40), kind=kLoop, calls=%fused_computation.450 | loop fusion | flops 41943040 | bytes 73400320 | tf_op jit(solution)/shard_map/convert_element_type | solution.py:797
  1233.8 6.0 multiply_add_fusion
  1239.8 5.1 copy.345
  1250.0 5.9 fusion.160
  (810 shorter events, 246.0 us)
Async XLA Ops:
  8.0 125.3 %reduce-scatter.4.cloned.1.call-start = ((), (), s32[]{:S(2)}) async-start(), calls=%async_computation.3 | async-start | bytes 5898240 | tf_op jit(solution)/shard_map/reduce_scatter | solution.py:510
  27.1 21.1 %copy-start.162 = (pred[1,4,8,128]{3,1,2,0:T(4,128)(4,1)}, pred[1,4,8,128]{3,1,2,0:T(4,128)(4,1)S(1)}, u32[]{:S(2)}) copy-start(pred[1,4,8,128]{3,1,2,0:T(4,128)(4,1)S(1)} %copy.375) | copy-start | bytes 12292
  54.2 122.0 %all-gather.11.cloned.1.call-start = ((), (), s32[]{:S(2)}) async-start(), calls=%async_computation.4 | async-start | bytes 10813440 | tf_op jit(solution)/shard_map/all_gather | solution.py:488
  56.2 198.1 %all-gather.13.cloned.1.call-start = ((), (), s32[]{:S(2)}) async-start(), calls=%async_computation.5 | async-start | bytes 8847360 | tf_op jit(solution)/shard_map/all_gather | solution.py:490
  57.4 275.2 %all-gather.15.cloned.1.call-start = ((), (), s32[]{:S(2)}) async-start(), calls=%async_computation.6 | async-start | bytes 8847360 | tf_op jit(solution)/shard_map/all_gather | solution.py:491
  60.0 74.5 %copy-start.18 = (f32[256,640]{1,0:T(8,128)S(1)}, f32[256,640]{1,0:T(8,128)}, u32[]{:S(2)}) copy-start(f32[256,640]{1,0:T(8,128)} %constant.152.clone) | copy-start | bytes 1966084
  60.0 349.9 %all-gather.17.cloned.1.call-start = ((), (), s32[]{:S(2)}) async-start(), calls=%async_computation.7 | async-start | bytes 2949120 | tf_op jit(solution)/shard_map/all_gather | solution.py:571
  60.9 163.2 %copy-start.216 = (pred[256]{0:T(512)(128)(4,1)}, pred[256]{0:T(512)(128)(4,1)S(1)}, u32[]{:S(2)}) copy-start(pred[256]{0:T(512)(128)(4,1)S(1)} %compare_reduce_fusion) | copy-start | bytes 772
  62.1 294.2 %copy-start.177 = (pred[1536]{0:T(1024)(128)(4,1)}, pred[1536]{0:T(1024)(128)(4,1)S(1)}, u32[]{:S(2)}) copy-start(pred[1536]{0:T(1024)(128)(4,1)S(1)} %iota_compare_fusion.2) | copy-start | bytes 4612
  62.9 72.3 %copy-start.158 = (f32[640]{0:T(1024)}, f32[640]{0:T(1024)S(1)}, u32[]{:S(2)}) copy-start(f32[640]{0:T(1024)S(1)} %get-tuple-element.212) | copy-start | bytes 7684
  62.9 72.3 %copy-start.160 = (f32[640]{0:T(1024)}, f32[640]{0:T(1024)S(1)}, u32[]{:S(2)}) copy-start(f32[640]{0:T(1024)S(1)} %get-tuple-element.214) | copy-start | bytes 7684
  62.9 298.1 %copy-start.156 = (f32[640]{0:T(1024)}, f32[640]{0:T(1024)S(1)}, u32[]{:S(2)}) copy-start(f32[640]{0:T(1024)S(1)} %get-tuple-element.207) | copy-start | bytes 7684
  135.2 65.8 %copy-start.218 = (f32[256]{0:T(256)}, f32[256]{0:T(256)S(1)}, u32[]{:S(2)}) copy-start(f32[256]{0:T(256)S(1)} %add_rsqrt_fusion.8) | copy-start | bytes 3076
  135.2 65.8 %copy-start.220 = (f32[256]{0:T(256)}, f32[256]{0:T(256)S(1)}, u32[]{:S(2)}) copy-start(f32[256]{0:T(256)S(1)} %add_rsqrt_fusion.9) | copy-start | bytes 3076
  135.6 70.0 %copy-start.88 = (bf16[256,640]{1,0:T(8,128)(2,1)}, bf16[256,640]{1,0:T(8,128)(2,1)S(1)}, u32[]{:S(2)}) copy-start(bf16[256,640]{1,0:T(8,128)(2,1)S(1)} %get-tuple-element.252) | copy-start | bytes 983044
  135.6 85.3 %copy-start.86 = (bf16[256,640]{1,0:T(8,128)(2,1)}, bf16[256,640]{1,0:T(8,128)(2,1)S(1)}, u32[]{:S(2)}) copy-start(bf16[256,640]{1,0:T(8,128)(2,1)S(1)} %get-tuple-element.251) | copy-start | bytes 983044
  205.6 10.7 slice-start.2
  228.7 25.6 %copy-start.180 = (f32[256]{0:T(256)}, f32[256]{0:T(256)S(1)}, u32[]{:S(2)}) copy-start(f32[256]{0:T(256)S(1)} %broadcast_multiply_fusion.28) | copy-start | bytes 3076
  230.4 23.9 %copy-start.198 = (f32[256]{0:T(256)}, f32[256]{0:T(256)S(1)}, u32[]{:S(2)}) copy-start(f32[256]{0:T(256)S(1)} %add_rsqrt_fusion.7) | copy-start | bytes 3076
  339.5 9.1 copy-start.217
  339.5 10.8 copy-start.182
  340.9 9.5 copy-start.209
  348.6 7.7 slice-start.8
  357.5 18.2 %copy-start.164 = (f32[256]{0:T(256)}, f32[256]{0:T(256)S(1)}, u32[]{:S(2)}) copy-start(f32[256]{0:T(256)S(1)} %broadcast_multiply_fusion.21) | copy-start | bytes 3076
  359.2 16.5 %copy-start.189 = (f32[256]{0:T(256)}, f32[256]{0:T(256)S(1)}, u32[]{:S(2)}) copy-start(f32[256]{0:T(256)S(1)} %add_rsqrt_fusion) | copy-start | bytes 3076
  377.3 67.7 %all-gather.19.cloned.1.call-start = ((), (), s32[]{:S(2)}) async-start(), calls=%async_computation.8 | async-start | bytes 2949120 | tf_op jit(solution)/shard_map/all_gather | solution.py:572
  378.1 246.1 %reduce-scatter.8.cloned.1.call-start = ((), (), s32[]{:S(2)}) async-start(), calls=%async_computation.10 | async-start | bytes 2949120 | tf_op jit(solution)/shard_map/reduce_scatter | solution.py:614
  587.4 36.8 %copy-start.165 = (f32[256]{0:T(256)S(1)}, f32[256]{0:T(256)}, u32[]{:S(2)}) copy-start(f32[256]{0:T(256)} %copy-done.164) | copy-start | bytes 3076
  587.4 36.8 %copy-start.190 = (f32[256]{0:T(256)S(1)}, f32[256]{0:T(256)}, u32[]{:S(2)}) copy-start(f32[256]{0:T(256)} %copy-done.189) | copy-start | bytes 3076
  587.4 38.9 %copy-start.178 = (pred[1536]{0:T(1024)(128)(4,1)S(1)}, pred[1536]{0:T(1024)(128)(4,1)}, u32[]{:S(2)}) copy-start(pred[1536]{0:T(1024)(128)(4,1)} %copy-done.177) | copy-start | bytes 4612
  587.4 76.0 %reduce-scatter.6.cloned.1.call-start = ((), (), s32[]{:S(2)}) async-start(), calls=%async_computation.9 | async-start | bytes 2949120 | tf_op jit(solution)/shard_map/reduce_scatter | solution.py:611
  588.0 386.5 %all-gather.21.cloned.1.call-start = ((), (), s32[]{:S(2)}) async-start(), calls=%async_computation.11 | async-start | bytes 5898240 | tf_op jit(solution)/shard_map/all_gather | solution.py:709
  626.3 37.0 %copy-start.226 = (f32[256]{0:T(256)}, f32[256]{0:T(256)S(1)}, u32[]{:S(2)}) copy-start(f32[256]{0:T(256)S(1)} %broadcast_multiply_fusion.17) | copy-start | bytes 3076
  626.4 37.0 %copy-start.228 = (f32[256]{0:T(256)}, f32[256]{0:T(256)S(1)}, u32[]{:S(2)}) copy-start(f32[256]{0:T(256)S(1)} %broadcast_multiply_fusion.18) | copy-start | bytes 3076
  629.8 33.6 %copy-start.168 = (f32[256]{0:T(256)S(1)}, f32[256]{0:T(256)}, u32[]{:S(2)}) copy-start(f32[256]{0:T(256)} %copy-done.167) | copy-start | bytes 3076
  629.8 33.6 %copy-start.193 = (f32[256]{0:T(256)S(1)}, f32[256]{0:T(256)}, u32[]{:S(2)}) copy-start(f32[256]{0:T(256)} %copy-done.192) | copy-start | bytes 3076
  693.8 7.8 copy-start.122
  693.8 14.5 %slice-start.12 = ((s8[7864320]{0:T(1024)(128)(4,1)}), s8[4194304]{0:T(1024)(128)(4,1)S(1)}, s32[]{:S(2)}) async-start(s8[7864320]{0:T(1024)(128)(4,1)} %bitcast.428), calls=%async_computation.26 | async-start | bytes 8388608
  700.3 8.1 slice-start.13
  703.2 9.6 copy-start.71
  705.4 7.5 copy-start.76
  731.2 9.2 copy-start.125
  745.1 289.8 %all-gather.23.cloned.1.call-start = ((), (), s32[]{:S(2)}) async-start(), calls=%async_computation.13 | async-start | bytes 2457600 | tf_op jit(solution)/shard_map/all_gather | solution.py:725
  831.5 143.0 %copy-start.163 = (pred[1,4,8,128]{3,1,2,0:T(4,128)(4,1)S(1)}, pred[1,4,8,128]{3,1,2,0:T(4,128)(4,1)}, u32[]{:S(2)}) copy-start(pred[1,4,8,128]{3,1,2,0:T(4,128)(4,1)} %copy-done.162) | copy-start | bytes 12292
  974.5 164.7 %all-reduce.4.cloned.1.call-start = ((), (), s32[]{:S(2)}) async-start(), calls=%async_computation.12 | async-start | bytes 10485760 | tf_op jit(solution)/shard_map/psum | solution.py:748
  1038.5 108.6 %copy-start.246 = (f32[2]{0:T(128)S(1)}, f32[2]{0:T(128)}, u32[]{:S(2)}) copy-start(f32[2]{0:T(128)} %get-tuple-element.270) | copy-start | bytes 28
  1145.0 47.2 %copy-start.63 = (f32[2,640,384]{1,2,0:T(8,128)S(1)}, f32[2,640,384]{1,2,0:T(8,128)}, u32[]{:S(2)}) copy-start(f32[2,640,384]{1,2,0:T(8,128)} %copy.340) | copy-start | bytes 5898244
  1206.2 27.5 %copy-start.24 = (f32[4096,160]{1,0:T(8,128)S(1)}, f32[4096,160]{1,0:T(8,128)}, u32[]{:S(2)}) copy-start(f32[4096,160]{1,0:T(8,128)} %copy.341) | copy-start | bytes 7864324
  (225 other events, 638.7 us)
Sparse Core Ops, SparseCore 0:
  54.3 78.9 reduce-scatter.3
  377.5 32.4 all-gather.16
  412.2 32.8 all-gather.18
  587.5 36.6 reduce-scatter.7
  626.9 36.4 reduce-scatter.5
  745.2 54.9 all-gather.20
  974.6 33.0 all-gather.22
  1019.3 119.7 all-reduce.3
Sparse Core Ops, SparseCore 1:
  58.1 118.0 all-gather.10
  178.2 76.0 all-gather.12
  256.4 76.1 all-gather.14

commit v3 on v2

--- a/solution.py
+++ b/solution.py
@@ -110,7 +110,6 @@
     q_in, kv_in, queries, key_rows, value_rows, log_total, mixed_low, allowed = kept
     tokens = q_in.shape[0]
     width = block.shape[1] // 4
-    out_weight_grad = dot_cols(grad_low, mixed_low)
     mixed_grad = jnp.dot(
         grad_low, block[:, 3 * width :], preferred_element_type=jnp.float32
     ).astype(jnp.bfloat16)
@@ -138,11 +137,10 @@
     pair_low = jnp.concatenate(
         [key_grad.reshape(tokens, width), value_grad.reshape(tokens, width)], axis=1
     ).astype(jnp.bfloat16)
-    block_grad = (dot_cols(q_in, query_low), dot_cols(kv_in, pair_low), out_weight_grad)
     return (
         dot_rows(query_low, block[:, :width]),
         dot_rows(pair_low, block[:, width : 3 * width]),
-        block_grad,
+        (q_in, query_low, kv_in, pair_low, grad_low, mixed_low),
     )
 
 
@@ -275,10 +273,266 @@
     )
 
 
+def gather_kernel(
+    f_shard, a_pair, f_full, a_full, local_sem, fz_send, fz_recv, fp_send, fp_recv, fs_send, fs_recv,
+    az_send, az_recv, ap_send, ap_recv, as_send, as_recv,
+):
+    dp, wide = lax.axis_index("dp"), lax.axis_index("wide")
+    level, core = wide // 2, wide % 2
+    row, col = dp // 2, dp % 2
+    sibling = (dp, level * 2 + 1 - core)
+    beside, across = row * 2 + 1 - col, (1 - row) * 2 + col
+    peers = (beside, across, (1 - row) * 2 + 1 - col)
+    half = a_pair.shape[2]
+
+    barrier = pltpu.get_barrier_semaphore()
+
+    def greet(device):
+        pl.semaphore_signal(barrier, inc=1, device_id=device, device_id_type=MESH)
+
+    for device in [sibling] + [(p, wide) for p in peers]:
+        greet(device)
+    can = (level < 3, level > 0)
+    step = (1, -1)
+    for d in range(2):
+        pl.when(can[d])(functools.partial(greet, (dp, (level + step[d]) * 2 + core)))
+    pl.semaphore_wait(barrier, 4 + can[0].astype(jnp.int32) + can[1].astype(jnp.int32))
+
+    def remote(src, dst, send, recv, device):
+        return pltpu.make_async_remote_copy(
+            src_ref=src, dst_ref=dst, send_sem=send, recv_sem=recv, device_id=device, device_id_type=MESH
+        )
+
+    def f_at(part, source):
+        return f_full.at[pl.ds(2 * part, 2), source * 2 + core, (col, row)[part]]
+
+    def f_other(part, source):
+        return f_full.at[pl.ds(2 * part, 2), source * 2 + core, 1 - (col, row)[part]]
+
+    def a_at(owner, source, side=core):
+        return a_full.at[
+            :, owner * 4 + source, :, pl.ds(pl.multiple_of(side * half, 128), half)
+        ]
+
+    def source_of(d, t):
+        return level - step[d] * t
+
+    def valid(d, t):
+        return (level >= t, level <= 3 - t)[d]
+
+    def chain_f(d, t, part):
+        source = source_of(d, t)
+        src = f_shard.at[pl.ds(2 * part, 2), (col, row)[part]] if t == 0 else f_at(part, source)
+        device = (dp, (level + step[d]) * 2 + core)
+        return remote(src, f_at(part, source), fz_send.at[d, t, part], fz_recv.at[d, t, part], device)
+
+    def chain_a(d, t):
+        source = source_of(d, t)
+        src = a_pair if t == 0 else a_at(dp, source)
+        device = (dp, (level + step[d]) * 2 + core)
+        return remote(src, a_at(dp, source), az_send.at[d, t], az_recv.at[d, t], device)
+
+    def chain(d, t):
+        return [chain_a(d, t), chain_f(d, t, 0), chain_f(d, t, 1)]
+
+    def plane_f(d, t, part):
+        at = f_at(part, source_of(d, t))
+        device = ((beside, across)[part], wide)
+        return remote(at, at, fp_send.at[d, t - 1, part], fp_recv.at[d, t - 1, part], device)
+
+    def plane_a(d, t, slot, p):
+        source = source_of(d, t)
+        src = a_pair if t == 0 else a_at(dp, source)
+        return remote(src, a_at(dp, source), ap_send.at[slot, p], ap_recv.at[slot, p], (peers[p], wide))
+
+    def pair_f(d, t, slot, other, part):
+        at = (f_other if other else f_at)(part, source_of(d, t))
+        return remote(at, at, fs_send.at[slot, other, part], fs_recv.at[slot, other, part], sibling)
+
+    def pair_a(owner, d, t, slot, p):
+        source = source_of(d, t)
+        src = a_pair if (t == 0 and p == 3) else a_at(owner, source)
+        return remote(src, a_at(owner, source), as_send.at[slot, p], as_recv.at[slot, p], sibling)
+
+    items = [(d, t) for t in (1, 2, 3) for d in range(2)]
+
+    def slot_of(d, t):
+        return 1 + 2 * (t - 1) + d
+
+    def start(copies):
+        for copy in copies:
+            copy.start()
+
+    for d in range(2):
+        pl.when(can[d])(lambda d=d: start(chain(d, 0)))
+    own = [
+        pltpu.make_async_copy(f_shard, f_full.at[:, wide], local_sem.at[0]),
+        pltpu.make_async_copy(a_pair, a_at(dp, level), local_sem.at[1]),
+    ]
+    start(own)
+    start([plane_a(0, 0, 0, p) for p in range(3)])
+    own_pair = [
+        remote(f_shard, f_full.at[:, wide], fs_send.at[0, 0, 0], fs_recv.at[0, 0, 0], sibling),
+        pair_a(dp, 0, 0, 0, 3),
+    ]
+    start(own_pair)
+
+    for d, t in items:
+
+        def arrived(d=d, t=t):
+            chain_a(d, t - 1).wait_recv()
+            if t < 3:
+                pl.when(can[d])(lambda: chain_a(d, t).start())
+            start([plane_a(d, t, slot_of(d, t), p) for p in range(3)])
+            pair_a(dp, d, t, slot_of(d, t), 3).start()
+
+        pl.when(valid(d, t))(arrived)
+    for d, t in items:
+
+        def arrived_f(d=d, t=t):
+            for part in range(2):
+                chain_f(d, t - 1, part).wait_recv()
+                if t < 3:
+                    pl.when(can[d])(lambda part=part: chain_f(d, t, part).start())
+                plane_f(d, t, part).start()
+                pair_f(d, t, slot_of(d, t), 0, part).start()
+
+        pl.when(valid(d, t))(arrived_f)
+
+    for p in range(3):
+        plane_a(0, 0, 0, p).wait_recv()
+        pair_a(peers[p], 0, 0, 0, p).start()
+    for d, t in items:
+
+        def spread(d=d, t=t):
+            for part in range(2):
+                plane_f(d, t, part).wait_recv()
+                pair_f(d, t, slot_of(d, t), 1, part).start()
+            for p in range(3):
+                plane_a(d, t, slot_of(d, t), p).wait_recv()
+                pair_a(peers[p], d, t, slot_of(d, t), p).start()
+
+        pl.when(valid(d, t))(spread)
+
+    for copy in own:
+        copy.wait()
+    for copy in own_pair:
+        copy.wait()
+    for p in range(3):
+        plane_a(0, 0, 0, p).wait_send()
+        pair_a(peers[p], 0, 0, 0, p).wait()
+    for d in range(2):
+
+        def sent(d=d):
+            for copy in chain(d, 0):
+                copy.wait_send()
+
+        pl.when(can[d])(sent)
+    for d, t in items:
+
+        def done(d=d, t=t):
+            slot = slot_of(d, t)
+            if t < 3:
+
+                def passed():
+                    for copy in chain(d, t):
+                        copy.wait_send()
+
+                pl.when(can[d])(passed)
+            for part in range(2):
+                plane_f(d, t, part).wait_send()
+                pair_f(d, t, slot, 0, part).wait()
+                pair_f(d, t, slot, 1, part).wait()
+            for p in range(3):
+                plane_a(d, t, slot, p).wait_send()
+            for p in range(4):
+                pair_a(peers[p] if p < 3 else dp, d, t, slot, p).wait()
+
+        pl.when(valid(d, t))(done)
+
+
+def weights_of(f_shard, a_pair, cid):
+    hbm = pl.BlockSpec(memory_space=pltpu.HBM)
+    dma = pltpu.SemaphoreType.DMA
+    kinds, _, lines, width = f_shard.shape
+    blocks, rows, half = a_pair.shape
+    return pl.pallas_call(
+        gather_kernel,
+        out_shape=(
+            jax.ShapeDtypeStruct((kinds, 8, 2, lines, width), jnp.bfloat16),
+            jax.ShapeDtypeStruct((blocks, 16, rows, half * 2), jnp.bfloat16),
+        ),
+        in_specs=[hbm, hbm],
+        out_specs=(hbm, hbm),
+        scratch_shapes=[
+            dma((2,)),
+            dma((2, 3, 2)), dma((2, 3, 2)),
+            dma((2, 3, 2)), dma((2, 3, 2)),
+            dma((7, 2, 2)), dma((7, 2, 2)),
+            dma((2, 3)), dma((2, 3)),
+            dma((7, 3)), dma((7, 3)),
+            dma((7, 4)), dma((7, 4)),
+        ],
+        compiler_params=pltpu.CompilerParams(collective_id=cid, has_side_effects=True),
+        name="gather_weights",
+    )(f_shard, a_pair)
+
+
+def attn_weight_kernel(count, *refs):
+    *inputs, out = refs
+    width = inputs[1].shape[1]
+    spans = ((0, width), (width, 3 * width), (3 * width, 4 * width))
+    for index, (first, last) in enumerate(spans):
+        total = 0.0
+        for n in range(count):
+            total += dot_cols(inputs[6 * n + 2 * index][...], inputs[6 * n + 2 * index + 1][...])
+        out[:, first:last] = total.astype(out.dtype)
+
+
+def attn_weight_grad(uses, kind):
+    return pl.pallas_call(
+        functools.partial(attn_weight_kernel, len(uses)),
+        out_shape=jax.ShapeDtypeStruct((uses[0][0].shape[1], 4 * uses[0][1].shape[1]), kind),
+        compiler_params=pltpu.CompilerParams(vmem_limit_bytes=48 << 20),
+        name="attn_weight_grad",
+    )(*[value for use in uses for value in use])
+
+
+def hidden_weight_kernel(small, left, left_small, right, right_small, out):
+    total = dot_cols(left[...], right[...])
+    if small:
+        extra = dot_cols(left_small[...], right_small[...])
+        total += jnp.where(pl.program_id(0) < small, extra, 0.0)
+    out[...] = total.astype(out.dtype)
+
+
+def hidden_weight_grad(parts, kind):
+    (left, right), second = parts[0], parts[-1]
+    tokens, units = left.shape
+    block = math.gcd(second[0].shape[1], 512)
+    small = second[0].shape[1] // block if len(parts) > 1 else 0
+    whole = lambda value: pl.BlockSpec(value.shape, lambda i: (0, 0))
+    last = second[0].shape[1] // block - 1
+    return pl.pallas_call(
+        functools.partial(hidden_weight_kernel, small),
+        out_shape=jax.ShapeDtypeStruct((units, right.shape[1]), kind),
+        grid=(units // block,),
+        in_specs=[
+            pl.BlockSpec((tokens, block), lambda i: (0, i)),
+            pl.BlockSpec((tokens, block), lambda i: (0, jnp.minimum(i, last))),
+            whole(right),
+            whole(second[1]),
+        ],
+        out_specs=pl.BlockSpec((block, right.shape[1]), lambda i: (i, 0)),
+        compiler_params=pltpu.CompilerParams(vmem_limit_bytes=48 << 20),
+        name="hidden_weight_grad",
+    )(left, second[0], right, second[1])
+
+
 def reduce_kernel(*refs):
-    hidden, attn, (hidden_out, attn_out) = refs[:4], refs[4], refs[5:7]
-    own_f, own_a, sib_f, sib_a, plane_f, plane_a, far_f, far_a = refs[7:15]
-    load_sem, pair_send, pair_recv, plane_send, plane_recv, far_send, far_recv = refs[15:]
+    hidden, attn, (hidden_out, attn_out) = refs[:4], refs[4:7], refs[7:9]
+    own_f, own_a, sib_f, sib_a, plane_f, plane_a, far_f, far_a = refs[9:17]
+    load_sem, pair_send, pair_recv, plane_send, plane_recv, far_send, far_recv = refs[17:]
     f32 = jnp.float32
     dp, wide = lax.axis_index("dp"), lax.axis_index("wide")
     level, core = wide // 2, wide % 2
@@ -299,6 +553,11 @@
         )
         copy.start()
         return copy
+
+    half = attn[0].shape[3] // 2
+
+    def columns(side):
+        return pl.ds(pl.multiple_of(side * half, 128), half)
 
     pair, loads = [], []
     for j in range(4):
@@ -310,18 +569,24 @@
             load = pltpu.make_async_copy(hidden[k].at[mine], own_f.at[j, k], load_sem.at[j, k])
             load.start()
             loads.append(load)
-        pair.append(
-            remote(attn.at[:, theirs], sib_a.at[j], pair_send.at[j, 4], pair_recv.at[j, 4], sibling)
-        )
-        load = pltpu.make_async_copy(attn.at[:, mine], own_a.at[j], load_sem.at[j, 4])
-        load.start()
-        loads.append(load)
+        for i in range(3):
+            pair.append(
+                remote(
+                    attn[i].at[:, far[j], :, columns(1 - core)], sib_a.at[j, i], pair_send.at[j, 4 + i],
+                    pair_recv.at[j, 4 + i], sibling,
+                )
+            )
+            load = pltpu.make_async_copy(
+                attn[i].at[:, far[j], :, columns(core)], own_a.at[j, i], load_sem.at[j, 4 + i]
+            )
+            load.start()
+            loads.append(load)
 
     plane = []
     for j in range(4):
-        for index in range(5):
-            loads[5 * j + index].wait()
-            pair[5 * j + index].wait_recv()
+        for index in range(7):
+            loads[7 * j + index].wait()
+            pair[7 * j + index].wait_recv()
 
         def add_f(k, carry):
             for q in range(4):
@@ -331,7 +596,8 @@
         lax.fori_loop(0, 4, add_f, 0)
 
         def add_a(q, carry):
-            own_a[j, q] = (own_a[j, q].astype(f32) + sib_a[j, q].astype(f32)).astype(jnp.bfloat16)
+            for i in range(3):
+                own_a[j, i, q] = (own_a[j, i, q].astype(f32) + sib_a[j, i, q].astype(f32)).astype(jnp.bfloat16)
             return carry
 
         lax.fori_loop(0, 4, add_a, 0)
@@ -340,7 +606,7 @@
             sent.append(
                 (
                     remote(own_f.at[j, :, peer], plane_f.at[j, p], plane_send.at[j, p, 0], plane_recv.at[j, p, 0], (peer, wide)),
-                    remote(own_a.at[j, peer], plane_a.at[j, p], plane_send.at[j, p, 1], plane_recv.at[j, p, 1], (peer, wide)),
+                    remote(own_a.at[j, :, peer], plane_a.at[j, p], plane_send.at[j, p, 1], plane_recv.at[j, p, 1], (peer, wide)),
                 )
             )
         plane.append(sent)
@@ -358,7 +624,7 @@
             return total
 
         def total_a():
-            total = own_a[j, dp].astype(f32)
+            total = own_a[j, :, dp].astype(f32)
             for p in range(3):
                 total += plane_a[j, p].astype(f32)
             return total
@@ -409,7 +675,8 @@
 
 def reduced(hidden, attn, cid):
     _, _, rows, width = hidden[0].shape
-    lines = attn.shape[2]
+    _, _, lines, columns = attn[0].shape
+    block = (3, lines, columns // 2)
     bf = jnp.bfloat16
     hbm = pl.BlockSpec(memory_space=pltpu.HBM)
     vmem = pl.BlockSpec(memory_space=pltpu.VMEM)
@@ -418,24 +685,83 @@
         reduce_kernel,
         out_shape=(
             jax.ShapeDtypeStruct((4, rows, width), jnp.float32),
-            jax.ShapeDtypeStruct((lines, 128), jnp.float32),
+            jax.ShapeDtypeStruct(block, jnp.float32),
         ),
-        in_specs=[hbm] * 5,
+        in_specs=[hbm] * 7,
         out_specs=(vmem, vmem),
         scratch_shapes=[
             pltpu.VMEM((4, 4, 4, rows, width), bf),
-            pltpu.VMEM((4, 4, lines, 128), bf),
+            pltpu.VMEM((4, 3, 4) + block[1:], bf),
             pltpu.VMEM((4, 4, 4, rows, width), bf),
-            pltpu.VMEM((4, 4, lines, 128), bf),
+            pltpu.VMEM((4, 3, 4) + block[1:], bf),
             pltpu.VMEM((4, 3, 4, rows, width), bf),
-            pltpu.VMEM((4, 3, lines, 128), bf),
+            pltpu.VMEM((4, 3) + block, bf),
             pltpu.VMEM((3, 4, rows, width), bf),
-            pltpu.VMEM((3, lines, 128), bf),
-            dma((4, 5)), dma((4, 5)), dma((4, 5)), dma((4, 3, 2)), dma((4, 3, 2)), dma((3, 2)), dma((3, 2)),
+            pltpu.VMEM((3,) + block, bf),
+            dma((4, 7)), dma((4, 7)), dma((4, 7)), dma((4, 3, 2)), dma((4, 3, 2)), dma((3, 2)), dma((3, 2)),
         ],
-        compiler_params=pltpu.CompilerParams(collective_id=cid, has_side_effects=True, vmem_limit_bytes=56 << 20),
+        compiler_params=pltpu.CompilerParams(
+            collective_id=cid, has_side_effects=True, vmem_limit_bytes=56 << 20
+        ),
         name="reduce_grads",
-    )(*hidden, attn)
+    )(*hidden, *attn)
+
+
+def total_kernel(own, out, pair, plane, far, pair_send, pair_recv, plane_send, plane_recv, far_send, far_recv):
+    dp, wide = lax.axis_index("dp"), lax.axis_index("wide")
+    level, core = wide // 2, wide % 2
+    row, col = dp // 2, dp % 2
+    sibling = (dp, level * 2 + 1 - core)
+    beside = (row * 2 + 1 - col, (1 - row) * 2 + col, (1 - row) * 2 + 1 - col)
+    above = [lax.rem(level + 1 + j, 4) for j in range(3)]
+    barrier = pltpu.get_barrier_semaphore()
+    partners = [sibling] + [(p, wide) for p in beside] + [(dp, a * 2 + core) for a in above]
+    for device in partners:
+        pl.semaphore_signal(barrier, inc=1, device_id=device, device_id_type=MESH)
+    pl.semaphore_wait(barrier, len(partners))
+
+    def exchange(buffer, mine, value, others, devices, send, recv):
+        buffer[mine] = value
+        copies = [
+            pltpu.make_async_remote_copy(
+                src_ref=buffer.at[mine], dst_ref=buffer.at[mine], send_sem=send.at[n], recv_sem=recv.at[mine],
+                device_id=device, device_id_type=MESH,
+            )
+            for n, device in enumerate(devices)
+        ]
+        for copy in copies:
+            copy.start()
+        for other, device in zip(others, devices):
+            pltpu.make_async_remote_copy(
+                src_ref=buffer.at[mine], dst_ref=buffer.at[other], send_sem=send.at[0], recv_sem=recv.at[other],
+                device_id=device, device_id_type=MESH,
+            ).wait_recv()
+        total = buffer[0]
+        for n in range(1, buffer.shape[0]):
+            total += buffer[n]
+        for copy in copies:
+            copy.wait_send()
+        return total
+
+    total = exchange(pair, core, own[...], [1 - core], [sibling], pair_send, pair_recv)
+    total = exchange(plane, dp, total, beside, [(p, wide) for p in beside], plane_send, plane_recv)
+    out[...] = exchange(far, level, total, above, [(dp, a * 2 + core) for a in above], far_send, far_recv)
+
+
+def total_of(own, cid):
+    dma = pltpu.SemaphoreType.DMA
+    vmem = lambda n: pltpu.VMEM((n,) + own.shape, own.dtype)
+    return pl.pallas_call(
+        total_kernel,
+        out_shape=jax.ShapeDtypeStruct(own.shape, own.dtype),
+        in_specs=[pl.BlockSpec(memory_space=pltpu.VMEM)],
+        out_specs=pl.BlockSpec(memory_space=pltpu.VMEM),
+        scratch_shapes=[
+            vmem(2), vmem(4), vmem(4), dma((1,)), dma((2,)), dma((3,)), dma((4,)), dma((3,)), dma((4,)),
+        ],
+        compiler_params=pltpu.CompilerParams(collective_id=cid, has_side_effects=True),
+        name="total_small",
+    )(own)
 
 
 def adamw(weight, first_m, second_m, grad_item, step_rate):
@@ -485,11 +811,30 @@
     vocab_shard = embed_master.shape[0]
     planes = (dp_count, wide_count) == (4, 8)
     link_type = jnp.bfloat16 if planes else jnp.float32
-    attn_full = lax.all_gather(attn_master.astype(jnp.bfloat16), ("dp", "wide"), axis=1, tiled=True)
-    up_full, down_full = (
-        lax.all_gather(up_master.astype(jnp.bfloat16), "wide", axis=2, tiled=True),
-        lax.all_gather(down_master.astype(jnp.bfloat16), "wide", axis=1, tiled=True),
-    )
+    core = wide_at % 2
+    swap = [(place, place ^ 1) for place in range(wide_count)]
+    hidden_shards = jnp.stack(
+        [up_master[0].T, down_master[0], up_master[1].T, down_master[1]]
+    ).astype(jnp.bfloat16)
+    attn_low = attn_master.astype(jnp.bfloat16)
+    if planes:
+        half = attn_low.shape[2] // 2
+        other_low = lax.ppermute(attn_low, "wide", swap)
+        pair_rows = jnp.concatenate(
+            [jnp.where(core > 0, other_low, attn_low), jnp.where(core > 0, attn_low, other_low)],
+            axis=1,
+        )
+        hidden_full, attn_full = weights_of(
+            hidden_shards.reshape(4, 2, -1, model_width),
+            lax.dynamic_slice_in_dim(pair_rows, core * half, half, 2),
+            2,
+        )
+        hidden_full = hidden_full.reshape(4, -1, model_width)
+        attn_full = attn_full.reshape(3, model_width, -1)
+    else:
+        attn_full = lax.all_gather(attn_low, ("dp", "wide"), axis=1, tiled=True)
+        hidden_full = lax.all_gather(hidden_shards, "wide", axis=1, tiled=True)
+    up_full, down_full = hidden_full[0::2], hidden_full[1::2]
     table_local = embed_master.astype(jnp.bfloat16)
     group_start = dp_at * wide_count * seq_dev
     own_start = group_start + wide_at * seq_dev
@@ -526,7 +871,7 @@
     src_hidden = src_in + src_att
     sff_val, sff_stats = norm_at(src_hidden, 1)
     sff_low = sff_val.astype(jnp.bfloat16)
-    src_inner = jnp.dot(sff_low, up_full[0], preferred_element_type=jnp.float32)
+    src_inner = dot_rows(sff_low, up_full[0])
     tgt_val, tgt_stats = norm_at(tgt_in, 3)
     tgt_low = tgt_val.astype(jnp.bfloat16)
     tgt_att, tgt_kept = attn_forward(tgt_low, tgt_low, attn_full[1], causal_mask, seq_dev)
@@ -535,7 +880,7 @@
     cross_low = cross_val.astype(jnp.bfloat16)
     passes = []
     final_list = []
-    pass_units = (up_full.shape[2], up_full.shape[2] // 2)
+    pass_units = (up_full.shape[1], up_full.shape[1] // 2)
     for pass_index in range(2):
         held = pass_units[pass_index]
         enc_out, enc_active, enc_act = ffn_pass(
@@ -547,7 +892,7 @@
         crossed = tgt_hidden + x_att
         dff_val, dff_stats = norm_at(crossed, 5)
         dff_low = dff_val.astype(jnp.bfloat16)
-        dec_inner = jnp.dot(dff_low, up_full[1, :, :held], preferred_element_type=jnp.float32)
+        dec_inner = dot_rows(dff_low, up_full[1, :held])
         dec_out, dec_active, dec_act = ffn_pass(
             crossed, dec_inner, down_full[1, :held], pass_widths[pass_index]
         )
@@ -647,13 +992,13 @@
         out_grad = backward_layer_norm(final_grads[pass_index], fin_stats, 6)
         out_low = out_grad.astype(jnp.bfloat16)
         held = pass_units[pass_index]
-        down_grads[1].append(dot_cols(dec_act, out_low))
+        down_grads[1].append((dec_act, out_low))
         dec_low = jnp.where(
             dec_active, dot_rows(out_low, down_full[1, :held]), 0.0
         ).astype(jnp.bfloat16)
-        up_grads[1].append(dot_cols(dec_low, dff_low))
+        up_grads[1].append((dec_low, dff_low))
         crossed_grad = out_grad + backward_layer_norm(
-            dot_rows(dec_low, up_full[1, :, :held]), dff_stats, 5
+            jnp.dot(dec_low, up_full[1, :held], preferred_element_type=jnp.float32), dff_stats, 5
         )
         query_in, memory_in, block_grad = attention_backward_pass(
             x_kept, crossed_grad.astype(jnp.bfloat16), attn_full[2]
@@ -663,7 +1008,7 @@
         cross_grad = cross_grad + query_in
         enc_grad = backward_layer_norm(memory_in, mem_stats, 2)
         enc_low = enc_grad.astype(jnp.bfloat16)
-        down_grads[0].append(dot_cols(enc_act, enc_low))
+        down_grads[0].append((enc_act, enc_low))
         src_inner_grad = src_inner_grad + jnp.pad(
             jnp.where(enc_active, dot_rows(enc_low, down_full[0, :held]), 0.0),
             ((0, 0), (0, src_inner.shape[1] - held)),
@@ -671,9 +1016,9 @@
         source_hidden_gradient = source_hidden_gradient + enc_grad
     tgt_hidden_grad = tgt_hidden_grad + backward_layer_norm(cross_grad, cross_stats, 4)
     src_inner_low = src_inner_grad.astype(jnp.bfloat16)
-    up_grads[0].append(dot_cols(src_inner_low, sff_low))
+    up_grads[0].append((src_inner_low, sff_low))
     source_hidden_gradient = source_hidden_gradient + backward_layer_norm(
-        dot_rows(src_inner_low, up_full[0]), sff_stats, 1
+        jnp.dot(src_inner_low, up_full[0], preferred_element_type=jnp.float32), sff_stats, 1
     )
     tq_in, tkv_in, tgt_weight = attention_backward_pass(
         tgt_kept, tgt_hidden_grad.astype(jnp.bfloat16), attn_full[1]
@@ -685,23 +1030,14 @@
     source_input_gradient = source_hidden_gradient + backward_layer_norm(
         source_query_input + source_key_value_input, source_norm_statistics, 0
     )
-    def joined(parts):
-        whole, *rest = parts
-        if rest:
-            half = rest[0].shape[0]
-            whole = jnp.concatenate([whole[:half] + rest[0], whole[half:]])
-        return whole
-
-    hidden_grads = [joined(p) for p in (down_grads[1], up_grads[1], down_grads[0], up_grads[0])]
-    cross_pair = tuple(first + second for first, second in zip(*cross_weight))
-    shards = dp_count * wide_count
-    attn_grad = jnp.stack(
-        [
-            jnp.concatenate(block, axis=1).astype(link_type).reshape(shards, -1, 128)
-            for block in (source_norm_weight, tgt_weight, cross_pair)
-        ],
-        axis=1,
-    )
+    hidden_grads = [
+        hidden_weight_grad(parts, link_type)
+        for parts in (down_grads[1], up_grads[1], down_grads[0], up_grads[0])
+    ]
+    attn_grads = [
+        attn_weight_grad(uses, link_type)
+        for uses in ([source_norm_weight], [tgt_weight], cross_weight)
+    ]
     norm_grad = jnp.stack(gain_parts + shift_parts)
     embed_low = (
         math.sqrt(model_width) * jnp.concatenate([source_input_gradient, tgt_in_grad], axis=0)
@@ -713,13 +1049,18 @@
         jnp.where(inside_rows[:, None], spread_rows.astype(jnp.float32), 0.0)
     )
     if planes:
-        hidden_part, attn_shard = reduced(
-            [
-                part.astype(link_type).reshape(wide_count, dp_count, -1, model_width)
-                for part in hidden_grads
-            ],
-            attn_grad.reshape(dp_count, wide_count, -1, 128),
+        hidden_part, attn_part = reduced(
+            [part.reshape(wide_count, dp_count, -1, model_width) for part in hidden_grads],
+            [part.reshape(4, 4, -1, part.shape[1]) for part in attn_grads],
             1,
+        )
+        lines = attn_master.shape[1]
+        mine = lax.dynamic_slice_in_dim(attn_part, core * lines, lines, 1)
+        other = lax.ppermute(
+            lax.dynamic_slice_in_dim(attn_part, (1 - core) * lines, lines, 1), "wide", swap
+        )
+        attn_shard = jnp.concatenate(
+            [jnp.where(core > 0, other, mine), jnp.where(core > 0, mine, other)], axis=2
         )
         hidden_sum = jnp.moveaxis(
             lax.all_gather(hidden_part.astype(link_type), "dp"), 0, 1
@@ -737,21 +1078,23 @@
         )
         square_part = jnp.sum(hidden_sum * hidden_sum) / dp_count
         attn_shard = lax.psum_scatter(
-            lax.psum_scatter(
-                attn_grad.reshape(-1, 128), "dp", scatter_dimension=0, tiled=True
-            ),
-            "wide",
-            scatter_dimension=0,
-            tiled=True,
-        )
-    attn_shard = attn_shard.reshape(attn_master.shape)
+            jnp.stack(attn_grads), ("dp", "wide"), scatter_dimension=1, tiled=True
+        )
     embed_sum = lax.psum(embed_part.astype(jnp.bfloat16), "dp").astype(jnp.float32)
     down_sum = jnp.stack([hidden_sum[2], hidden_sum[0]])
     up_sum = jnp.stack([hidden_sum[3].T, hidden_sum[1].T])
     square_part += (
         jnp.sum(attn_shard * attn_shard) + jnp.sum(embed_sum * embed_sum) / dp_count
     )
-    square_all, norm_sum, losses = lax.psum((square_part, norm_grad, loss_own), ("dp", "wide"))
+    if planes:
+        flat = jnp.concatenate([norm_grad.reshape(-1), loss_own, square_part.reshape(1)])
+        flat = total_of(jnp.pad(flat, (0, -flat.size % 1024)).reshape(-1, 128), 3).reshape(-1)
+        norm_sum = flat[: norm_grad.size].reshape(norm_grad.shape)
+        losses, square_all = flat[norm_grad.size :][:2], flat[norm_grad.size + 2]
+    else:
+        square_all, norm_sum, losses = lax.psum(
+            (square_part, norm_grad, loss_own), ("dp", "wide")
+        )
     grad_norm = jnp.sqrt(square_all + jnp.sum(norm_sum * norm_sum))
     clip_scale = clip_limit / jnp.maximum(grad_norm, clip_limit)
     attn_new, attn_m_new, attn_v_new = adamw(

time: 1270 us -> 1130 us (0.89)
  waiting for transfers between devices: 431 us -> 226 us
  Pallas kernels: 252 us -> 434 us
  local copies, waits for them, and re-layouts: 211 us -> 170 us
  blocking collectives: 55.1 us -> 14.7 us
  matrix products: 130 us -> 98.3 us
    pallas_call x0 -> x9, Pallas kernels: none -> 181 us  [the longest x1 145 us: weights_of(): pl.pallas_call(gather_kernel, out_shape=(jax.ShapeDtypeStruct((kinds, 8,...]
    all_gather x3 -> x0, waiting for transfers between devices: 133 us -> none  [the longest x1 72.8 us: local(): lax.all_gather(down_master.astype(jnp.bfloat16), 'wide', axis=1, tiled=True)]
    reduce_scatter x1, waiting for transfers between devices: 70.3 us -> 0.02 us  [local(): lax.psum_scatter(jnp.where(inside[:, None], found_rows, 0.0).astype(jnp.b...]
    psum x1 -> x0, blocking collectives: 40.4 us -> none  [local(): lax.psum((square_part, norm_grad, loss_own), ('dp', 'wide'))]
    dot_general x22 -> x3, matrix products: 42.6 us -> 6.89 us  [the longest x2 5.25 us: local(): jnp.dot(dec_low, up_full[1, :held], preferred_element_type=jnp.float32)]
    slice x4 -> x6, local copies, waits for them, and re-layouts: 29.2 us -> 15.2 us  [the longest x1 6.35 us: local(): up_full, down_full = (hidden_full[0::2], hidden_full[1::2])]
    unnamed x549 -> x469, local copies, waits for them, and re-layouts: 88.2 us -> 76.4 us
  transfers between devices with their start and end apart: 11 -> 10, of which waited for: 9 -> 5; matrix products, arithmetic and copies ran while one was open for 18% -> 10% of each run, Pallas kernels for 11% -> 28%
where the time goes in v3:
time: 1130 us; the launch traced here: 1120 us
  Pallas kernels  434 us (38%)
  waiting for transfers between devices  226 us (20%)
  local copies, waits for them, and re-layouts  170 us (15%)
  other arithmetic  151 us (13%)
  matrix products  98.3 us (9%)
  between operations  23.1 us (2%)
  blocking collectives  14.7 us (1%)
    pallas_call x1, Pallas kernels, weights_of(): pl.pallas_call(gather_kernel, out_shape=(jax.ShapeDtypeStruct((kinds, 8,...  145 us
    pallas_call x1, Pallas kernels, reduced(): pl.pallas_call(reduce_kernel, out_shape=(jax.ShapeDtypeStruct((4, rows, w...  140 us
    psum x1, waiting for transfers between devices, local(): lax.psum(embed_part.astype(jnp.bfloat16), 'dp').astype(jnp.float32)  99.7 us
    unnamed x469, local copies, waits for them, and re-layouts  76.4 us
    pallas_call x1, Pallas kernels, head_grads(): pl.pallas_call(functools.partial(head_grads_kernel, block), out_shape=(ja...  63.2 us
    pallas_call x1, Pallas kernels, head_stats(): pl.pallas_call(functools.partial(head_stats_kernel, block), out_shape=(ja...  48.9 us
    dot_general x19, matrix products, dot_rows(): lax.dot_general(left, right, (((1,), (1,)), ((), ())), preferred_element_...  46.5 us
    scatter-add x1, other arithmetic, local(): table_grad.at[jnp.clip(local_ids, 0, vocab_shard - 1)]  37.8 us
  transfers between devices with their start and end apart: 10, of which 5 were waited for; matrix products, arithmetic and copies ran while one was open for 10% of the time, Pallas kernels for 28%

profile of v3, /device:TPU:0, one launch (start us, length us, event | category | flops | bytes accessed | tf_op | source)
XLA Modules:
  0.0 1119.0 jit_solution(6029235465688046678)
XLA Ops:
  8.7 9.1 copy.313
  17.7 7.8 copy.314.table_ref
  26.3 21.1 %gather_fusion = bf16[4096,640]{1,0:T(8,128)(2,1)} fusion(bf16[4096,640]{1,0:T(8,128)(2,1)} %copy.314.table_ref, s32[4096]{0:T(1024)S(1)} %broadcast_clamp_fusion), kind=kCustom, calls=%fused_computation | custom fusion | bytes 10502144 | tf_op jit(solution)/shard_map/jit(_take)/gather | solution.py:852
  47.4 5.9 select_convert_fusion
  65.5 145.0 %gather_weights.1 = (bf16[4,8,2,192,640]{4,3,2,1,0:T(8,128)(2,1)}, bf16[3,16,40,2048]{3,2,1,0:T(8,128)(2,1)}) custom-call(bf16[4,2,192,640]{3,2,1,0:T(8,128)(2,1)} %pad_maximum_fusion.f_shard, bf16[3,40,1024]{2,1,0:T(8,128)(2,1)} %fusion.100.a_pair), custom_call_target="tpu_custom_call" | custom-call | tf_op jit(solution)/shard_map/gather_weights/pallas_call | solution.py:459
  210.5 6.3 fusion.131
  216.8 4.2 copy-done.67
  221.1 6.4 fusion.130
  279.4 3.0 select_convert_fusion.1
  290.0 28.6 %all-gather.8.cloned.1.call-done = bf16[2048,640]{1,0:T(8,128)(2,1)} async-done(((bf16[256,640]{1,0:T(8,128)(2,1)}), bf16[2048,640]{1,0:T(8,128)(2,1)}) %all-gather.8.cloned.1.call-update) | async-done | bytes 2621456 | tf_op jit(solution)/shard_map/all_gather | solution.py:916
  318.6 3.5 constant_dynamic-update-slice_fusion.1
  322.1 31.7 %all-gather.10.cloned.1.call-done = bf16[2048,640]{1,0:T(8,128)(2,1)} async-done(((bf16[256,640]{1,0:T(8,128)(2,1)}), bf16[2048,640]{1,0:T(8,128)(2,1)}) %all-gather.10.cloned.1.call-update) | async-done | bytes 2621456 | tf_op jit(solution)/shard_map/all_gather | solution.py:917
  353.7 3.5 constant_dynamic-update-slice_fusion.z_ref
  357.2 48.9 %head_stats.1 = (bf16[4096,4096]{1,0:T(8,128)(2,1)}, f32[8,4,4096]{2,1,0:T(4,128)}) custom-call(s32[1]{0:T(128)} %bitcast.36.offset_ref, bf16[4096,640]{1,0:T(8,128)(2,1)} %copy.314.table_ref, bf16[4096,640]{1,0:T(8,128)(2,1)} %constant_dynamic-update-slice_fusion.z_ref, s32[1,4096]{1,0:T(1,128)} %bitcast.444), custom_call_target="tpu_custom_call" | custom-call | tf_op jit(solution)/shard_map/head_stats/pallas_call | solution.py:181
  409.6 14.7 %all-gather.2 = f32[8,4,4096]{2,1,0:T(4,128)S(1)} all-gather(f32[1,4,4096]{2,1,0:T(4,128)S(1)} %maximum_bitcast_fusion), channel_id=2, replica_groups=mesh['dp'=4,'wide'=8] {'wide'}, dimensions={0}, use_global_device_ids=true | all-gather | bytes 589824 | tf_op jit(solution)/shard_map/all_gather | solution.py:33
  426.9 63.2 %head_grads.1 = (bf16[4096,640]{1,0:T(8,128)(2,1)}, f32[4096,640]{1,0:T(8,128)}) custom-call(s32[1]{0:T(128)} %bitcast.36.offset_ref, bf16[4096,4096]{1,0:T(8,128)(2,1)} %get-tuple-element.33.exp_ref, bf16[640,4096]{1,0:T(8,128)(2,1)} %bitcast.337, bf16[4096,640]{1,0:T(8,128)(2,1)} %constant_dynamic-update-slice_fusion.z_ref, s32[1,4096]{1,0:T(1,128)} %bitcast.445, ...), custom_call_target="tpu_custom_call" | custom-call | tf_op jit(solution)/shard_map/head_grads/pallas_call | solution.py:245
  490.1 5.3 fusion.132
  496.6 35.6 %reduce-scatter.8.cloned.1.call-done = bf16[256,640]{1,0:T(8,128)(2,1)} async-done(((bf16[2048,640]{1,0:T(8,128)(2,1)}), bf16[256,640]{1,0:T(8,128)(2,1)}) %reduce-scatter.8.cloned.1.call-update) | async-done | bytes 327696 | tf_op jit(solution)/shard_map/reduce_scatter | solution.py:959
  537.6 3.6 multiply_reduce_fusion.7
  541.3 29.6 %reduce-scatter.6.cloned.1.call-done = bf16[256,640]{1,0:T(8,128)(2,1)} async-done(((bf16[2048,640]{1,0:T(8,128)(2,1)}), bf16[256,640]{1,0:T(8,128)(2,1)}) %reduce-scatter.6.cloned.1.call-update) | async-done | bytes 327696 | tf_op jit(solution)/shard_map/reduce_scatter | solution.py:956
  570.9 3.5 fusion.128
  575.8 4.8 fusion.11.left
  617.8 3.1 multiply_reduce_fusion.12
  628.4 3.9 fusion.10.left.left_small
  661.2 2.9 multiply_reduce_fusion.6
  677.8 5.1 hidden_weight_grad.4
  683.0 5.1 hidden_weight_grad.5
  688.1 5.1 hidden_weight_grad.6
  705.9 3.1 attn_weight_grad.5
  709.0 140.3 %reduce_grads.1 = (f32[4,96,640]{2,1,0:T(8,128)}, f32[3,40,1024]{2,1,0:T(8,128)}) custom-call(bf16[8,4,96,640]{3,2,1,0:T(8,128)(2,1)} %bitcast.339, bf16[8,4,96,640]{3,2,1,0:T(8,128)(2,1)} %bitcast.340, bf16[8,4,96,640]{3,2,1,0:T(8,128)(2,1)} %bitcast.341, bf16[8,4,96,640]{3,2,1,0:T(8,128)(2,1)} %bitcast.334, bf16[4,4,40,2048]{3,2,1,0:T(8,128)(2,1)} %bitcast.335, ...), custom_call_target="tpu_custom_call" | custom-call | tf_op jit(solution)/shard_map/reduce_grads/pallas_call | solution.py:684
  849.3 3.0 fusion.134
  852.5 37.8 %scatter_custom_fusion = f32[4096,640]{1,0:T(8,128)} fusion(f32[4096,640]{1,0:T(8,128)} %get-tuple-element.38, s32[4096]{0:T(1024)} %bitcast.451, bf16[4096,640]{1,0:T(8,128)(2,1)} %all-gather.12.cloned.1.call-done, f32[]{:T(128)} %constant.67.clone.1, pred[4096]{0:T(1024)(128)(4,1)S(1)} %bitcast.459), kind=kCustom, calls=%fused_computation.10 | custom fusion | flops 7864320 | bytes 15733248 | tf_op jit(solution)/shard_map/scatter-add | solution.py:1048
  890.3 6.9 convert_element_type.399
  898.5 2.8 copy.371
  901.3 3.1 copy.369
  904.4 2.8 copy.368
  907.2 5.0 copy.372
  917.6 99.7 %all-reduce.4.cloned.1.call-done = bf16[4096,640]{1,0:T(8,128)(2,1)} async-done(((bf16[4096,640]{1,0:T(8,128)(2,1)}), bf16[4096,640]{1,0:T(8,128)(2,1)}) %all-reduce.4.cloned.1.call-update) | async-done | bytes 5242896 | tf_op jit(solution)/shard_map/psum | solution.py:1083
  1017.3 5.8 fusion.2
  1025.8 13.7 %total_small.1 = f32[72,128]{1,0:T(8,128)} custom-call(f32[72,128]{1,0:T(8,128)} %pad_bitcast_fusion.own), custom_call_target="tpu_custom_call" | custom-call | tf_op jit(solution)/shard_map/total_small/pallas_call | solution.py:754
  1045.5 7.1 fusion.119
  1052.5 2.8 copy.373
  1055.3 2.8 copy.374
  1061.0 27.5 %fusion.114 = (bf16[4096,640]{1,0:T(8,128)(2,1)}, f32[4096,640]{1,0:T(8,128)}, f32[4096,640]{1,0:T(8,128)}, f32[4096,640]{1,0:T(8,128)}) fusion(f32[4096,640]{1,0:T(8,128)} %param.39, bf16[4096,640]{1,0:T(8,128)(2,1)} %all-reduce.4.cloned.1.call-done, f32[]{:T(128)S(6)} %div.254, f32[4096,640]{1,0:T(8,128)} %param.41, f32[4096,640]{1,0:T(8,128)} %param.40), kind=kLoop, calls=%fused_computation.398 | loop fusion | flops 41943040 | bytes 73400320 | tf_op jit(solution)/shard_map/convert_element_type | solution.py:1140
  1088.5 6.0 multiply_add_fusion
  1094.5 5.1 copy.376
  1101.9 3.0 fusion.121
  1105.5 5.3 fusion.117
  (738 shorter events, 201.8 us)
Async XLA Ops:
  7.2 220.2 %reduce-scatter.4.cloned.1.call-start = ((), (), s32[]{:S(2)}) async-start(), calls=%async_computation.3 | async-start | bytes 5898240 | tf_op jit(solution)/shard_map/reduce_scatter | solution.py:855
  26.3 21.1 %copy-start.157 = (pred[1,4,8,128]{3,1,2,0:T(4,128)(4,1)}, pred[1,4,8,128]{3,1,2,0:T(4,128)(4,1)S(1)}, u32[]{:S(2)}) copy-start(pred[1,4,8,128]{3,1,2,0:T(4,128)(4,1)S(1)} %copy.399) | copy-start | bytes 12292
  53.3 265.3 %all-gather.8.cloned.1.call-start = ((), (), s32[]{:S(2)}) async-start(), calls=%async_computation.4 | async-start | bytes 2949120 | tf_op jit(solution)/shard_map/all_gather | solution.py:916
  54.4 9.2 collective-permute-start
  59.9 169.5 %copy-start.153 = (f32[640]{0:T(1024)}, f32[640]{0:T(1024)S(1)}, u32[]{:S(2)}) copy-start(f32[640]{0:T(1024)S(1)} %get-tuple-element.214) | copy-start | bytes 7684
  59.9 169.5 %copy-start.155 = (f32[640]{0:T(1024)}, f32[640]{0:T(1024)S(1)}, u32[]{:S(2)}) copy-start(f32[640]{0:T(1024)S(1)} %get-tuple-element.218) | copy-start | bytes 7684
  63.6 146.9 %copy-start.188 = (pred[256]{0:T(512)(128)(4,1)}, pred[256]{0:T(512)(128)(4,1)S(1)}, u32[]{:S(2)}) copy-start(pred[256]{0:T(512)(128)(4,1)S(1)} %compare_reduce_fusion) | copy-start | bytes 772
  210.5 10.6 copy-start.67
  228.7 14.6 %copy-start.55 = (f32[512,640]{1,0:T(8,128)}, f32[512,640]{1,0:T(8,128)S(1)}, u32[]{:S(2)}) copy-start(f32[512,640]{1,0:T(8,128)S(1)} %convert_element_type.310) | copy-start | bytes 3932164
  238.4 14.5 %copy-start.175 = (f32[256]{0:T(256)}, f32[256]{0:T(256)S(1)}, u32[]{:S(2)}) copy-start(f32[256]{0:T(256)S(1)} %add_rsqrt_fusion.5) | copy-start | bytes 3076
  242.0 5.4 slice-start
  253.5 5.7 copy-start.17
  253.5 13.0 %copy-start.15 = (bf16[256,640]{1,0:T(8,128)(2,1)}, bf16[256,640]{1,0:T(8,128)(2,1)S(1)}, u32[]{:S(2)}) copy-start(bf16[256,640]{1,0:T(8,128)(2,1)S(1)} %get-tuple-element.302.refs_8_) | copy-start | bytes 983044
  266.3 7.7 copy-start.177
  266.5 7.4 copy-start.198
  276.3 6.1 slice-start.10
  279.1 254.6 %copy-start.66 = (f32[256,640]{1,0:T(8,128)}, f32[256,640]{1,0:T(8,128)S(1)}, u32[]{:S(2)}) copy-start(f32[256,640]{1,0:T(8,128)S(1)} %get-tuple-element.339) | copy-start | bytes 1966084
  285.9 67.8 %all-gather.10.cloned.1.call-start = ((), (), s32[]{:S(2)}) async-start(), calls=%async_computation.5 | async-start | bytes 2949120 | tf_op jit(solution)/shard_map/all_gather | solution.py:917
  286.7 245.6 %reduce-scatter.8.cloned.1.call-start = ((), (), s32[]{:S(2)}) async-start(), calls=%async_computation.7 | async-start | bytes 2949120 | tf_op jit(solution)/shard_map/reduce_scatter | solution.py:959
  495.5 36.7 %copy-start.168 = (f32[256]{0:T(256)S(1)}, f32[256]{0:T(256)}, u32[]{:S(2)}) copy-start(f32[256]{0:T(256)} %copy-done.167) | copy-start | bytes 3076
  495.5 75.4 %reduce-scatter.6.cloned.1.call-start = ((), (), s32[]{:S(2)}) async-start(), calls=%async_computation.6 | async-start | bytes 2949120 | tf_op jit(solution)/shard_map/reduce_scatter | solution.py:956
  495.6 39.4 %copy-start.205 = (pred[1536]{0:T(1024)(128)(4,1)S(1)}, pred[1536]{0:T(1024)(128)(4,1)}, u32[]{:S(2)}) copy-start(pred[1536]{0:T(1024)(128)(4,1)} %iota_compare_fusion.2) | copy-start | bytes 4612
  496.1 356.3 %all-gather.12.cloned.1.call-start = ((), (), s32[]{:S(2)}) async-start(), calls=%async_computation.8 | async-start | bytes 5898240 | tf_op jit(solution)/shard_map/all_gather | solution.py:1045
  537.6 33.3 %copy-start.91 = (bf16[256,640]{1,0:T(8,128)(2,1)S(1)}, bf16[256,640]{1,0:T(8,128)(2,1)}, u32[]{:S(2)}) copy-start(bf16[256,640]{1,0:T(8,128)(2,1)} %reduce-scatter.8.cloned.1.call-done) | copy-start | bytes 983044
  537.6 33.3 %copy-start.166 = (f32[256]{0:T(256)S(1)}, f32[256]{0:T(256)}, u32[]{:S(2)}) copy-start(f32[256]{0:T(256)} %copy-done.165) | copy-start | bytes 3076
  570.9 9.7 slice-start.4
  574.4 19.3 %copy-start.13 = (bf16[256,640]{1,0:T(8,128)(2,1)}, bf16[256,640]{1,0:T(8,128)(2,1)S(1)}, u32[]{:S(2)}) copy-start(bf16[256,640]{1,0:T(8,128)(2,1)S(1)} %get-tuple-element.249.refs_10_) | copy-start | bytes 983044
  583.6 6.6 copy-start.19
  625.5 6.9 slice-start.6
  655.0 6.1 copy-start.154
  655.0 6.1 copy-start.156
  655.0 6.1 copy-start.170
  655.0 6.1 copy-start.172
  655.0 6.1 copy-start.191
  655.1 6.1 copy-start.193
  665.8 248.4 %all-gather.14.cloned.1.call-start = ((), (), s32[]{:S(2)}) async-start(), calls=%async_computation.10 | async-start | bytes 2457600 | tf_op jit(solution)/shard_map/all_gather | solution.py:1066
  677.8 5.1 copy-start.12
  677.8 5.1 copy-start.32
  677.8 5.1 copy-start.34
  677.8 5.1 copy-start.42
  683.0 5.1 copy-start.8
  683.0 5.1 copy-start.30
  683.0 5.1 copy-start.44
  709.0 143.4 %copy-start.158 = (pred[1,4,8,128]{3,1,2,0:T(4,128)(4,1)S(1)}, pred[1,4,8,128]{3,1,2,0:T(4,128)(4,1)}, u32[]{:S(2)}) copy-start(pred[1,4,8,128]{3,1,2,0:T(4,128)(4,1)} %copy-done.157) | copy-start | bytes 12292
  852.4 165.0 %all-reduce.4.cloned.1.call-start = ((), (), s32[]{:S(2)}) async-start(), calls=%async_computation.9 | async-start | bytes 10485760 | tf_op jit(solution)/shard_map/psum | solution.py:1083
  898.2 15.0 %collective-permute-start.1 = (f32[3,20,1024]{2,1,0:T(8,128)S(1)}, f32[3,20,1024]{2,1,0:T(8,128)S(1)}, u32[]{:S(2)}, u32[]{:S(2)}) collective-permute-start(f32[3,20,1024]{2,1,0:T(8,128)S(1)} %constant_dynamic-slice_fusion), channel_id=1, source_target_pairs={{0,1},{1,0},{2,3},{3,2},{4,5},{5,4},{6,7},{7,6},{8,9},{9,8},{10,11... | collective-permute-start | bytes 737288 | tf_op jit(solution)/shard_map/ppermute | solution.py:1059
  1061.0 27.5 %copy-start.63 = (f32[4096,160]{1,0:T(8,128)S(1)}, f32[4096,160]{1,0:T(8,128)}, u32[]{:S(2)}) copy-start(f32[4096,160]{1,0:T(8,128)} %copy.372) | copy-start | bytes 7864324
  1105.5 5.3 copy-start.1
  (186 other events, 450.3 us)
Sparse Core Ops, SparseCore 0:
  53.5 90.3 reduce-scatter.3
  286.0 32.5 all-gather.7
  320.8 32.8 all-gather.9
  495.6 36.5 reduce-scatter.7
  534.4 36.4 reduce-scatter.5
  665.9 55.5 all-gather.11
  852.5 33.0 all-gather.13
  897.3 119.9 all-reduce.3
